TPU v7x, 128 devices: a whole 4x4x4 slice. The times are simulated.
128 devices in a mesh: gx: 4 (over x), gy: 4 (over z), gz: 8 (over y, core).
Axes of the slice: x: 4, y: 4, z: 4, core: 2. Of those that a mesh axis runs over, the one named last changes fastest.
Arguments:
- state: float32 [16, 32, 256, 256], P('gx', 'gy', 'gz'), may hold values from -6 to 6
- convection: bfloat16 [16, 32, 256, 4096], P('gx', 'gy', 'gz'), may hold values from -0.375 to 0.375
- inverse_mass: bfloat16 [16, 32, 256, 4096], P('gx', 'gy', 'gz'), may hold values from -0.75 to 0.75
- face_coupling: bfloat16 [96, 64], replicated, may hold values from -0.3125 to 0.3125
- lower_bound: float32 [16, 32, 256, 256], P('gx', 'gy', 'gz'), may hold values from -3 to -1
- upper_bound: float32 [16, 32, 256, 256], P('gx', 'gy', 'gz'), may hold values from 1 to 3
- new_owner: int32 [128, 1024, 1], P(('gx', 'gy', 'gz')), may hold values from 0 to 127; in each aligned block of 1024 rows (0 to 1023, 1024 to 2047, ..., all dimensions but the last counted through in order) at most 16 rows name the same one
Outputs:
- handed: float32 [262144, 256], P(('gx', 'gy', 'gz'))
Inputs may be any that keep to these rules, and one draw needn't show every extreme that they name: `new_owner`: among the zones of one device no owner is named more than 16 times, a bound that some block reaches.
All inputs are finite; a program needn't handle non-finite values.
Results may differ from a plain program's by a relative error of at most 0.003.
Values may be sent and summed in bfloat16 or wider, within the bound.
No kernel may reach another device: no remote copies, remote signals or barrier semaphores. Data moves between devices by JAX's collectives and lax.ppermute only.
A program may use at most 128 MiB of HBM per device.

v0:
```python
import jax
import jax.numpy as jnp
from jax import lax
from jax.sharding import PartitionSpec as P

COMP = 4
DOFS = 64
STEPS = 2


HIGH = lax.Precision.HIGHEST


def padded(cells, sides, width):
    for axis, dim in sides:
        count = lax.axis_size(axis)
        ends = count - 1
        head = lax.slice_in_dim(cells, 0, width, axis=dim)
        tail = lax.slice_in_dim(cells, cells.shape[dim] - width, cells.shape[dim], axis=dim)
        cells = jnp.concatenate(
            [
                lax.ppermute(tail, axis, [(i, (i + 1) % count) for i in range(ends)]),
                cells,
                lax.ppermute(head, axis, [((i + 1) % count, i) for i in range(ends)]),
            ],
            axis=dim,
        )
    return cells


def face_tables(face_coupling):
    columns = jnp.arange(COMP * DOFS, dtype=jnp.int32)
    component = columns // DOFS
    local = columns % DOFS
    first = local // 16
    second = local // 4 % 4
    third = local % 4
    coords = (first, second, third)
    rests = (4 * second + third, 4 * first + third, 4 * first + second)
    outputs = jnp.arange(COMP * 16, dtype=jnp.int32)
    out_comp = outputs // 16
    out_face = outputs % 16

    def select(direction, level):
        match = (
            (coords[direction] == level)[:, None]
            & (component[:, None] == out_comp[None, :])
            & (rests[direction][:, None] == out_face[None, :])
        )
        return match.astype(jnp.float32)

    identity = jnp.eye(COMP, dtype=jnp.float32)

    def couple(face):
        block = face_coupling[16 * face : 16 * face + 16].astype(jnp.float32)
        return jnp.einsum("cd,fi->cfdi", identity, block).reshape(COMP * 16, COMP * DOFS)

    picks = []
    whole = []
    spreads = []
    blank = jnp.zeros((COMP * 16, COMP * DOFS), jnp.float32)
    for direction in range(3):
        upper_pick = select(direction, 3)
        lower_pick = select(direction, 0)
        before = couple(2 * direction)
        after = couple(2 * direction + 1)
        whole.append(jnp.dot(upper_pick, before, precision=HIGH).astype(jnp.bfloat16))
        whole.append(jnp.dot(lower_pick, after, precision=HIGH).astype(jnp.bfloat16))
        picks.append(jnp.concatenate([upper_pick, lower_pick], axis=1).astype(jnp.bfloat16))
        spreads.append(
            (
                jnp.concatenate([before, blank], axis=0).astype(jnp.bfloat16),
                jnp.concatenate([blank, after], axis=0).astype(jnp.bfloat16),
            )
        )
    return (picks, whole, spreads)


def apply_table(piece, table):
    width = piece.shape[-1]
    return jnp.dot(piece.reshape(-1, width), table, preferred_element_type=jnp.float32)


def face_flux(work, tables):
    picks, whole, spreads = tables
    ex, ey, ez = (work.shape[0], work.shape[1], work.shape[2])
    rows = work.reshape(ex * ey * ez, COMP * DOFS)

    def payload(direction):
        return (
            jnp.dot(rows, picks[direction], preferred_element_type=jnp.float32)
            .astype(jnp.bfloat16)
            .reshape(ex, ey, ez, COMP * 32)
        )

    along_x = padded(payload(0), (("gx", 0),), 1)
    along_y = padded(payload(1), (("gy", 1),), 1)
    along_z = padded(payload(2), (("gz", 2),), 1)
    flux = apply_table(along_x[0:ex], spreads[0][0])
    flux = flux + apply_table(along_x[2 : ex + 2], spreads[0][1])
    flux = flux + apply_table(along_y[:, 0:ey], spreads[1][0])
    flux = flux + apply_table(along_y[:, 2 : ey + 2], spreads[1][1])
    flux = flux + apply_table(along_z[:, :, 0:ez], spreads[2][0])
    flux = flux + apply_table(along_z[:, :, 2 : ez + 2], spreads[2][1])
    return flux


def remap_step(state, convection, inverse_mass, tables, lower_bound, upper_bound):
    ex, ey, ez, width = state.shape
    zones = ex * ey * ez
    work = state.astype(jnp.bfloat16)
    flux = face_flux(work, tables)
    conv = convection.reshape(zones, DOFS, DOFS)
    pushed = jnp.einsum(
        "ecj,eij->eci", work.reshape(zones, COMP, DOFS), conv, preferred_element_type=jnp.float32
    )
    rhs = (pushed + flux.reshape(zones, COMP, DOFS)).astype(jnp.bfloat16)
    inverse = inverse_mass.reshape(zones, DOFS, DOFS)
    change = jnp.einsum("ecj,eij->eci", rhs, inverse, preferred_element_type=jnp.float32)
    moved = state + change.reshape(ex, ey, ez, width)
    return jnp.minimum(jnp.maximum(moved, lower_bound), upper_bound)


def shards(state, convection, inverse_mass, face_coupling, lower_bound, upper_bound, new_owner):
    tables = face_tables(face_coupling)
    for step in range(STEPS):
        state = remap_step(state, convection, inverse_mass, tables, lower_bound, upper_bound)
    ex, ey, ez, width = state.shape
    zones = ex * ey * ez
    devices = lax.axis_size(("gx", "gy", "gz"))
    capacity = max(2, 2 * zones // devices)
    rows = state.reshape(zones, width)
    owner = new_owner[0, :, 0]
    onehot = (owner[:, None] == jnp.arange(devices, dtype=jnp.int32)[None, :]).astype(jnp.bfloat16)
    positions = jnp.arange(zones, dtype=jnp.int32)
    lower_tri = (positions[:, None] >= positions[None, :]).astype(jnp.bfloat16)
    running = jnp.dot(lower_tri, onehot, preferred_element_type=jnp.float32)
    rank = jnp.sum(running * onehot.astype(jnp.float32), axis=1).astype(jnp.int32) - 1
    target = owner * capacity + rank
    outgoing = jnp.zeros((devices * capacity, width), jnp.float32).at[target].set(rows)
    arrived = lax.all_to_all(
        outgoing.reshape(devices, capacity, width),
        ("gx", "gy", "gz"),
        split_axis=0,
        concat_axis=0,
        tiled=True,
    )
    return arrived.reshape(devices * capacity, width)


def solution(mesh):
    in_specs = (
        P("gx", "gy", "gz", None),
        P("gx", "gy", "gz", None),
        P("gx", "gy", "gz", None),
        P(),
        P("gx", "gy", "gz", None),
        P("gx", "gy", "gz", None),
        P(("gx", "gy", "gz"), None, None),
    )
    out_specs = P(("gx", "gy", "gz"), None)
    return jax.shard_map(shards, mesh=mesh, in_specs=in_specs, out_specs=out_specs, check_vma=False)
```

profile of v0, /device:TPU:1, one launch (start us, length us, event | category | flops | bytes accessed | tf_op | source)
XLA Modules:
  0.0 208.2 jit_solution(12061111938143978302)
XLA Ops:
  0.1 1.3 convert_element_type.88
  1.6 0.3 fusion.12
  2.1 4.4 %collective-permute-start.2 = (bf16[4,1,32,128]{3,2,1,0:T(8,128)(2,1)S(1)}, bf16[4,1,32,128]{3,2,1,0:T(8,128)(2,1)S(1)}, u32[]{:S(2)}, u32[]{:S(2)}) collective-permute-start(bf16[4,1,32,128]{3,2,1,0:T(8,128)(2,1)S(1)} %get-tuple-element.23), channel_id=1, source_target_pairs={{0,8},{8,16},{16,24},{1,9},{9,17},{17,25},{2,10},{10,18},{18,26},{... | collective-permute-start | bytes 98312 | tf_op jit(solution)/shard_map/ppermute | solution.py:22
  6.5 1.3 collective-permute-start.3
  7.8 0.3 fusion.13
  8.3 4.0 %collective-permute-start.4 = (bf16[4,8,1,128]{3,2,1,0:T(2,128)(2,1)S(1)}, bf16[4,8,1,128]{3,2,1,0:T(2,128)(2,1)S(1)}, u32[]{:S(2)}, u32[]{:S(2)}) collective-permute-start(bf16[4,8,1,128]{3,2,1,0:T(2,128)(2,1)S(1)} %get-tuple-element.27), channel_id=1, source_target_pairs={{0,1},{1,2},{2,3},{3,4},{4,5},{5,6},{6,7},{8,9},{9,10},{10,11},{11... | collective-permute-start | bytes 24584 | tf_op jit(solution)/shard_map/ppermute | solution.py:22
  12.4 1.9 collective-permute-start.5
  14.3 0.3 fusion.11
  14.7 3.1 %collective-permute-start = (bf16[1,8,32,128]{3,2,1,0:T(8,128)(2,1)S(1)}, bf16[1,8,32,128]{3,2,1,0:T(8,128)(2,1)S(1)}, u32[]{:S(2)}, u32[]{:S(2)}) collective-permute-start(bf16[1,8,32,128]{3,2,1,0:T(8,128)(2,1)S(1)} %bitcast.119), channel_id=1, source_target_pairs={{0,32},{32,64},{64,96},{1,33},{33,65},{65,97},{2,34},{34,66},{66,9... | collective-permute-start | bytes 196616 | tf_op jit(solution)/shard_map/ppermute | solution.py:22
  18.5 0.6 fusion.10
  19.4 0.6 compare_select_fusion
  20.2 1.4 reshape.279
  22.4 23.6 %reshape.280 = bf16[1024,64,64]{2,1,0:T(8,128)(2,1)} reshape(bf16[4,8,32,4096]{3,2,1,0:T(8,128)(2,1)} %param.8) | data formatting | bytes 16777216 | tf_op jit(solution)/shard_map/reshape | solution.py:113
  46.0 23.6 %reshape.298 = bf16[1024,64,64]{2,1,0:T(8,128)(2,1)} reshape(bf16[4,8,32,4096]{3,2,1,0:T(8,128)(2,1)} %param.9) | data formatting | bytes 16777216 | tf_op jit(solution)/shard_map/reshape | solution.py:118
  69.6 1.5 collective-permute-start.1
  71.3 0.3 fusion.23
  71.7 0.3 fusion.27
  72.1 0.3 fusion.31
  72.4 0.3 fusion.35
  72.7 1.9 collective-permute-done.1
  74.7 0.3 fusion.39
  75.0 0.4 fusion.8
  75.4 0.9 copy.55
  76.4 22.9 %fusion.16 = f32[1024,4,64]{2,1,0:T(4,128)} fusion(bf16[1024,64,64]{2,1,0:T(8,128)(2,1)} %reshape.298, f32[1024,4,64]{2,1,0:T(4,128)S(1)} %copy.55, bf16[1024,4,64]{2,1,0:T(4,128)(2,1)} %reshape.279, bf16[1024,64,64]{2,1,0:T(8,128)(2,1)} %reshape.280), kind=kOutput, calls=%fused_computation.30 | convolution fusion | flops 67633152 | bytes 19398656 | tf_op jit(solution)/shard_map/ecj,eij->eci/dot_general | solution.py:119
  99.2 2.6 %reshape.299 = f32[4,8,32,256]{3,2,1,0:T(8,128)S(1)} reshape(f32[1024,4,64]{2,1,0:T(4,128)} %fusion.16) | data formatting | bytes 2097152 | tf_op jit(solution)/shard_map/reshape | solution.py:120
  101.8 1.9 fusion.19
  104.3 0.3 convolution_convert_fusion
  104.6 1.4 reshape.300
  106.0 3.1 %collective-permute-start.6 = (bf16[1,8,32,128]{3,2,1,0:T(8,128)(2,1)S(1)}, bf16[1,8,32,128]{3,2,1,0:T(8,128)(2,1)S(1)}, u32[]{:S(2)}, u32[]{:S(2)}) collective-permute-start(bf16[1,8,32,128]{3,2,1,0:T(8,128)(2,1)S(1)} %bitcast.122), channel_id=1, source_target_pairs={{0,32},{32,64},{64,96},{1,33},{33,65},{65,97},{2,34},{34,66},{66,9... | collective-permute-start | bytes 196616 | tf_op jit(solution)/shard_map/ppermute | solution.py:22
  109.1 1.3 collective-permute-start.7
  110.5 5.4 %collective-permute-start.10 = (bf16[4,8,1,128]{3,2,1,0:T(2,128)(2,1)S(1)}, bf16[4,8,1,128]{3,2,1,0:T(2,128)(2,1)S(1)}, u32[]{:S(2)}, u32[]{:S(2)}) collective-permute-start(bf16[4,8,1,128]{3,2,1,0:T(2,128)(2,1)S(1)} %get-tuple-element.15), channel_id=1, source_target_pairs={{0,1},{1,2},{2,3},{3,4},{4,5},{5,6},{6,7},{8,9},{9,10},{10,11},{11... | collective-permute-start | bytes 24584 | tf_op jit(solution)/shard_map/ppermute | solution.py:22
  115.8 1.9 collective-permute-start.11
  117.8 4.3 %collective-permute-start.8 = (bf16[4,1,32,128]{3,2,1,0:T(8,128)(2,1)S(1)}, bf16[4,1,32,128]{3,2,1,0:T(8,128)(2,1)S(1)}, u32[]{:S(2)}, u32[]{:S(2)}) collective-permute-start(bf16[4,1,32,128]{3,2,1,0:T(8,128)(2,1)S(1)} %get-tuple-element.11), channel_id=1, source_target_pairs={{0,8},{8,16},{16,24},{1,9},{9,17},{17,25},{2,10},{10,18},{18,26},{... | collective-permute-start | bytes 98312 | tf_op jit(solution)/shard_map/ppermute | solution.py:22
  122.1 1.5 collective-permute-start.9
  123.8 1.1 fusion.25
  124.9 0.3 fusion.21
  125.3 1.7 collective-permute-done.9
  127.0 0.3 fusion.33
  127.3 0.3 fusion.29
  127.7 0.3 fusion.37
  128.1 0.4 fusion.4
  128.5 1.7 copy.56
  130.3 23.1 %fusion.17 = f32[1024,4,64]{2,1,0:T(4,128)} fusion(bf16[1024,64,64]{2,1,0:T(8,128)(2,1)} %reshape.298, f32[1024,4,64]{2,1,0:T(4,128)} %copy.56, bf16[1024,4,64]{2,1,0:T(4,128)(2,1)} %reshape.300, bf16[1024,64,64]{2,1,0:T(8,128)(2,1)} %reshape.280), kind=kOutput, calls=%fused_computation.31 | convolution fusion | flops 67633152 | bytes 19398656 | tf_op jit(solution)/shard_map/ecj,eij->eci/dot_general | solution.py:119
  153.3 2.5 %reshape.312 = f32[4,8,32,256]{3,2,1,0:T(8,128)S(1)} reshape(f32[1024,4,64]{2,1,0:T(4,128)} %fusion.17) | data formatting | bytes 2097152 | tf_op jit(solution)/shard_map/reshape | solution.py:120
  155.8 3.1 %maximum_minimum_fusion = f32[4,8,32,256]{3,2,1,0:T(8,128)} fusion(f32[4,8,32,256]{3,2,1,0:T(8,128)} %param.12, f32[4,8,32,256]{3,2,1,0:T(8,128)} %param.11, f32[4,8,32,256]{3,2,1,0:T(8,128)S(1)} %reshape.312, f32[4,8,32,256]{3,2,1,0:T(8,128)S(1)} %copy-done, f32[4,8,32,256]{3,2,1,0:T(8,128)S(1)} %reshape.299), kind=kLoop, calls=%fused_computation.26 | loop fusion | flops 1572864 | bytes 6291456 | tf_op jit(solution)/shard_map/min | solution.py:121
  158.9 5.8 %scatter_custom_fusion = f32[2048,256]{1,0:T(8,128)S(1)} fusion(s32[1024]{0:T(1024)} %bitcast.125, f32[1024,256]{1,0:T(8,128)} %bitcast.118, f32[]{:T(128)} %constant.91.clone.1), kind=kCustom, calls=%fused_computation.28 | custom fusion | bytes 2097664 | tf_op jit(solution)/shard_map/scatter | solution.py:140
  164.7 42.2 %all_to_all.5 = f32[128,16,256]{2,1,0:T(8,128)S(1)} all-to-all(f32[128,16,256]{2,1,0:T(8,128)S(1)} %bitcast.92), channel_id=1, replica_groups=mesh['gx'=4,'gy'=4,'gz'=8] {'gx','gy','gz'}, dimensions={0} | all-to-all | bytes 4194304 | tf_op jit(solution)/shard_map/all_to_all | solution.py:141
  206.9 1.3 copy.82
  (74 shorter events, 3.8 us)
Async XLA Ops:
  1.4 16.5 %copy-start.1 = (bf16[96,64]{0,1:T(8,128)(2,1)S(1)}, bf16[96,64]{0,1:T(8,128)(2,1)}, u32[]{:S(2)}) copy-start(bf16[96,64]{0,1:T(8,128)(2,1)} %param.10) | copy-start | bytes 36868
  1.6 6.2 %copy-start.5 = (pred[256,64]{0,1:T(32,128)(4,1)}, pred[256,64]{0,1:T(32,128)(4,1)S(1)}, u32[]{:S(2)}) copy-start(pred[256,64]{0,1:T(32,128)(4,1)S(1)} %get-tuple-element.48) | copy-start | bytes 49156
  1.6 16.9 %copy-start.7 = (s32[1,1024,1]{1,2,0:T(1,128)S(1)}, s32[1,1024,1]{1,2,0:T(1,128)}, u32[]{:S(2)}) copy-start(s32[1,1024,1]{1,2,0:T(1,128)} %param.13) | copy-start | bytes 12292
  2.1 69.9 %collective-permute-start.2 = (bf16[4,1,32,128]{3,2,1,0:T(8,128)(2,1)S(1)}, bf16[4,1,32,128]{3,2,1,0:T(8,128)(2,1)S(1)}, u32[]{:S(2)}, u32[]{:S(2)}) collective-permute-start(bf16[4,1,32,128]{3,2,1,0:T(8,128)(2,1)S(1)} %get-tuple-element.23), channel_id=1, source_target_pairs={{0,8},{8,16},{16,24},{1,9},{9,17},{17,25},{2,10},{10,18},{18,26},{... | collective-permute-start | bytes 98312 | tf_op jit(solution)/shard_map/ppermute | solution.py:22
  6.5 65.5 %collective-permute-start.3 = (bf16[4,1,32,128]{3,2,1,0:T(8,128)(2,1)S(1)}, bf16[4,1,32,128]{3,2,1,0:T(8,128)(2,1)S(1)}, u32[]{:S(2)}, u32[]{:S(2)}) collective-permute-start(bf16[4,1,32,128]{3,2,1,0:T(8,128)(2,1)S(1)} %get-tuple-element.24), channel_id=1, source_target_pairs={{8,0},{16,8},{24,16},{9,1},{17,9},{25,17},{10,2},{18,10},{26,18},{... | collective-permute-start | bytes 98312 | tf_op jit(solution)/shard_map/ppermute | solution.py:24
  8.3 61.3 %collective-permute-start.4 = (bf16[4,8,1,128]{3,2,1,0:T(2,128)(2,1)S(1)}, bf16[4,8,1,128]{3,2,1,0:T(2,128)(2,1)S(1)}, u32[]{:S(2)}, u32[]{:S(2)}) collective-permute-start(bf16[4,8,1,128]{3,2,1,0:T(2,128)(2,1)S(1)} %get-tuple-element.27), channel_id=1, source_target_pairs={{0,1},{1,2},{2,3},{3,4},{4,5},{5,6},{6,7},{8,9},{9,10},{10,11},{11... | collective-permute-start | bytes 24584 | tf_op jit(solution)/shard_map/ppermute | solution.py:22
  12.4 58.7 %collective-permute-start.5 = (bf16[4,8,1,128]{3,2,1,0:T(2,128)(2,1)S(1)}, bf16[4,8,1,128]{3,2,1,0:T(2,128)(2,1)S(1)}, u32[]{:S(2)}, u32[]{:S(2)}) collective-permute-start(bf16[4,8,1,128]{3,2,1,0:T(2,128)(2,1)S(1)} %get-tuple-element.28), channel_id=1, source_target_pairs={{1,0},{2,1},{3,2},{4,3},{5,4},{6,5},{7,6},{9,8},{10,9},{11,10},{12... | collective-permute-start | bytes 24584 | tf_op jit(solution)/shard_map/ppermute | solution.py:24
  14.7 58.0 %collective-permute-start = (bf16[1,8,32,128]{3,2,1,0:T(8,128)(2,1)S(1)}, bf16[1,8,32,128]{3,2,1,0:T(8,128)(2,1)S(1)}, u32[]{:S(2)}, u32[]{:S(2)}) collective-permute-start(bf16[1,8,32,128]{3,2,1,0:T(8,128)(2,1)S(1)} %bitcast.119), channel_id=1, source_target_pairs={{0,32},{32,64},{64,96},{1,33},{33,65},{65,97},{2,34},{34,66},{66,9... | collective-permute-start | bytes 196616 | tf_op jit(solution)/shard_map/ppermute | solution.py:22
  22.0 49.3 %copy-start.2 = (bf16[64,256]{1,0:T(8,128)(2,1)}, bf16[64,256]{1,0:T(8,128)(2,1)S(1)}, u32[]{:S(2)}) copy-start(bf16[64,256]{1,0:T(8,128)(2,1)S(1)} %reshape.296) | copy-start | bytes 98308
  22.1 49.6 %copy-start.4 = (bf16[64,256]{1,0:T(8,128)(2,1)}, bf16[64,256]{1,0:T(8,128)(2,1)S(1)}, u32[]{:S(2)}) copy-start(bf16[64,256]{1,0:T(8,128)(2,1)S(1)} %reshape.294) | copy-start | bytes 98308
  69.6 5.0 %collective-permute-start.1 = (bf16[1,8,32,128]{3,2,1,0:T(8,128)(2,1)S(1)}, bf16[1,8,32,128]{3,2,1,0:T(8,128)(2,1)S(1)}, u32[]{:S(2)}, u32[]{:S(2)}) collective-permute-start(bf16[1,8,32,128]{3,2,1,0:T(8,128)(2,1)S(1)} %bitcast.120), channel_id=1, source_target_pairs={{32,0},{64,32},{96,64},{33,1},{65,33},{97,65},{34,2},{66,34},{98,6... | collective-permute-start | bytes 196616 | tf_op jit(solution)/shard_map/ppermute | solution.py:24
  99.2 2.6 %copy-start = (f32[4,8,32,256]{3,2,1,0:T(8,128)S(1)}, f32[4,8,32,256]{3,2,1,0:T(8,128)}, u32[]{:S(2)}) copy-start(f32[4,8,32,256]{3,2,1,0:T(8,128)} %param.7) | copy-start | bytes 3145732
  101.8 2.5 %copy-start.6 = (pred[256,64]{0,1:T(32,128)(4,1)S(1)}, pred[256,64]{0,1:T(32,128)(4,1)}, u32[]{:S(2)}) copy-start(pred[256,64]{0,1:T(32,128)(4,1)} %copy-done.5) | copy-start | bytes 49156
  106.0 18.9 %copy-start.3 = (bf16[64,256]{1,0:T(8,128)(2,1)S(1)}, bf16[64,256]{1,0:T(8,128)(2,1)}, u32[]{:S(2)}) copy-start(bf16[64,256]{1,0:T(8,128)(2,1)} %copy-done.2) | copy-start | bytes 98308
  106.0 21.6 %collective-permute-start.6 = (bf16[1,8,32,128]{3,2,1,0:T(8,128)(2,1)S(1)}, bf16[1,8,32,128]{3,2,1,0:T(8,128)(2,1)S(1)}, u32[]{:S(2)}, u32[]{:S(2)}) collective-permute-start(bf16[1,8,32,128]{3,2,1,0:T(8,128)(2,1)S(1)} %bitcast.122), channel_id=1, source_target_pairs={{0,32},{32,64},{64,96},{1,33},{33,65},{65,97},{2,34},{34,66},{66,9... | collective-permute-start | bytes 196616 | tf_op jit(solution)/shard_map/ppermute | solution.py:22
  109.1 18.5 %collective-permute-start.7 = (bf16[1,8,32,128]{3,2,1,0:T(8,128)(2,1)S(1)}, bf16[1,8,32,128]{3,2,1,0:T(8,128)(2,1)S(1)}, u32[]{:S(2)}, u32[]{:S(2)}) collective-permute-start(bf16[1,8,32,128]{3,2,1,0:T(8,128)(2,1)S(1)} %bitcast.121), channel_id=1, source_target_pairs={{32,0},{64,32},{96,64},{33,1},{65,33},{97,65},{34,2},{66,34},{98,6... | collective-permute-start | bytes 196616 | tf_op jit(solution)/shard_map/ppermute | solution.py:24
  110.5 11.6 %collective-permute-start.10 = (bf16[4,8,1,128]{3,2,1,0:T(2,128)(2,1)S(1)}, bf16[4,8,1,128]{3,2,1,0:T(2,128)(2,1)S(1)}, u32[]{:S(2)}, u32[]{:S(2)}) collective-permute-start(bf16[4,8,1,128]{3,2,1,0:T(2,128)(2,1)S(1)} %get-tuple-element.15), channel_id=1, source_target_pairs={{0,1},{1,2},{2,3},{3,4},{4,5},{5,6},{6,7},{8,9},{9,10},{10,11},{11... | collective-permute-start | bytes 24584 | tf_op jit(solution)/shard_map/ppermute | solution.py:22
  115.8 7.8 %collective-permute-start.11 = (bf16[4,8,1,128]{3,2,1,0:T(2,128)(2,1)S(1)}, bf16[4,8,1,128]{3,2,1,0:T(2,128)(2,1)S(1)}, u32[]{:S(2)}, u32[]{:S(2)}) collective-permute-start(bf16[4,8,1,128]{3,2,1,0:T(2,128)(2,1)S(1)} %get-tuple-element.16), channel_id=1, source_target_pairs={{1,0},{2,1},{3,2},{4,3},{5,4},{6,5},{7,6},{9,8},{10,9},{11,10},{12... | collective-permute-start | bytes 24584 | tf_op jit(solution)/shard_map/ppermute | solution.py:24
  117.8 7.5 %collective-permute-start.8 = (bf16[4,1,32,128]{3,2,1,0:T(8,128)(2,1)S(1)}, bf16[4,1,32,128]{3,2,1,0:T(8,128)(2,1)S(1)}, u32[]{:S(2)}, u32[]{:S(2)}) collective-permute-start(bf16[4,1,32,128]{3,2,1,0:T(8,128)(2,1)S(1)} %get-tuple-element.11), channel_id=1, source_target_pairs={{0,8},{8,16},{16,24},{1,9},{9,17},{17,25},{2,10},{10,18},{18,26},{... | collective-permute-start | bytes 98312 | tf_op jit(solution)/shard_map/ppermute | solution.py:22
  122.1 4.9 %collective-permute-start.9 = (bf16[4,1,32,128]{3,2,1,0:T(8,128)(2,1)S(1)}, bf16[4,1,32,128]{3,2,1,0:T(8,128)(2,1)S(1)}, u32[]{:S(2)}, u32[]{:S(2)}) collective-permute-start(bf16[4,1,32,128]{3,2,1,0:T(8,128)(2,1)S(1)} %get-tuple-element.12), channel_id=1, source_target_pairs={{8,0},{16,8},{24,16},{9,1},{17,9},{25,17},{10,2},{18,10},{26,18},{... | collective-permute-start | bytes 98312 | tf_op jit(solution)/shard_map/ppermute | solution.py:24
where the time goes:
time: 210 us; the launch traced here: 208 us
  local copies, waits for them, and re-layouts  66.9 us (32%)
  matrix products  53.3 us (25%)
  blocking collectives  42.2 us (20%)
  starting transfers between devices  33.7 us (16%)
  other arithmetic  7.98 us (4%)
  waiting for transfers between devices  3.55 us (2%)
    dot_general x2, matrix products, remap_step(): jnp.einsum('ecj,eij->eci', rhs, inverse, preferred_element_type=jnp.float32)  45.9 us
    all_to_all x1, blocking collectives, shards(): lax.all_to_all(outgoing.reshape(devices, capacity, width), ('gx', 'gy', '...  42.2 us
    ppermute x6, starting transfers between devices, padded(): lax.ppermute(tail, axis, [(i, (i + 1) % count) for i in range(ends)])  24.3 us
    reshape x1, local copies, waits for them, and re-layouts, remap_step(): conv = convection.reshape(zones, DOFS, DOFS)  23.6 us
    reshape x1, local copies, waits for them, and re-layouts, remap_step(): inverse = inverse_mass.reshape(zones, DOFS, DOFS)  23.6 us
    ppermute x6, starting transfers between devices, padded(): lax.ppermute(head, axis, [((i + 1) % count, i) for i in range(ends)])  9.4 us
    scatter x1, local copies, waits for them, and re-layouts, shards(): jnp.zeros((devices * capacity, width), jnp.float32).at[target].set(rows)  5.78 us
    reshape x2, local copies, waits for them, and re-layouts, remap_step(): moved = state + change.reshape(ex, ey, ez, width)  5.04 us
  transfers between devices with their start and end apart: 12, of which 2 were waited for; matrix products, arithmetic and copies ran while one was open for 27% of the time, Pallas kernels for 0%

commit v1 on v0

v1 whole, which is shorter than its diff:
```python
import jax
import jax.numpy as jnp
import numpy as np
from jax import lax
from jax.experimental import pallas as pl
from jax.experimental.pallas import tpu as pltpu
from jax.sharding import PartitionSpec as P

COMP = 4
DOFS = 64
STEPS = 2
WIDTH = COMP * DOFS
EX, EY, EZ = 4, 8, 32
ZONES = EX * EY * EZ
PLANE = EY * EZ
TILE = 128
TILES = ZONES // TILE
ROWS = 8
FACE = COMP * 16
CAP = 16
AXES = ("gx", "gy", "gz")
F32 = jnp.float32
BF16 = jnp.bfloat16


def pick_table():
    table = np.zeros((6, COMP, 16, COMP, 4, 4, 4), np.float32)
    for c in range(COMP):
        for f in range(16):
            p, q = f // 4, f % 4
            for side, level in ((0, 3), (1, 0)):
                table[0 + side, c, f, c, level, p, q] = 1
                table[2 + side, c, f, c, p, level, q] = 1
                table[4 + side, c, f, c, p, q, level] = 1
    return table.reshape(6 * FACE, WIDTH)


def dot(a, b):
    return jnp.dot(a, b, preferred_element_type=F32)


def select_zones(zone_of, count):
    column = lax.broadcasted_iota(jnp.int32, (1, 128), 1)
    wanted = jnp.where(column < count, zone_of(column), -1)
    zone = lax.broadcasted_iota(jnp.int32, (ZONES, 128), 0)
    return jnp.where(zone == wanted, 1.0, 0.0).astype(BF16)


def place_zones(zone_of, count):
    row = lax.broadcasted_iota(jnp.int32, (128, 1), 0)
    wanted = jnp.where(row < count, zone_of(row), -1)
    zone = lax.broadcasted_iota(jnp.int32, (128, ZONES), 1)
    return jnp.where(zone == wanted, 1.0, 0.0).astype(BF16)


def y_zone(level):
    return lambda n: (n // EZ) * PLANE + level * EZ + n % EZ


def z_zone(level):
    return lambda n: n * EZ + level


SENDS = ((64, 256), (64, 256), (64, 128), (64, 128), (64, 128), (64, 128))


def write_faces(work, pick_ref, flags_ref, payload_ref, send_refs):
    payload = dot(pick_ref[...], work).astype(BF16)
    payload_ref[...] = payload

    def face(k):
        return payload[FACE * k : FACE * (k + 1)]

    pieces = (
        face(0)[:, ZONES - PLANE :].astype(F32),
        face(1)[:, :PLANE].astype(F32),
        dot(face(2), select_zones(y_zone(EY - 1), EX * EZ)),
        dot(face(3), select_zones(y_zone(0), EX * EZ)),
        dot(face(4), select_zones(z_zone(EZ - 1), EX * EY)),
        dot(face(5), select_zones(z_zone(0), EX * EY)),
    )
    for k in range(6):
        send_refs[k][...] = jnp.where(flags_ref[k] > 0, pieces[k], 0.0).astype(BF16)


def incoming_flux(payload_ref, halo_refs, spread_ref, incoming_ref, flux_ref):
    def face(k):
        return payload_ref[FACE * k : FACE * (k + 1), :]

    incoming_ref[0:FACE, 0:PLANE] = halo_refs[0][...]
    incoming_ref[0:FACE, PLANE:ZONES] = payload_ref[0:FACE, 0 : ZONES - PLANE]
    incoming_ref[FACE : 2 * FACE, 0 : ZONES - PLANE] = payload_ref[FACE : 2 * FACE, PLANE:ZONES]
    incoming_ref[FACE : 2 * FACE, ZONES - PLANE : ZONES] = halo_refs[1][...]
    zone = lax.broadcasted_iota(jnp.int32, (FACE, ZONES), 1)
    third = zone % EZ
    second = zone // EZ % EY
    cases = (
        (2, EZ, second == 0, y_zone(0), EX * EZ),
        (3, ZONES - EZ, second == EY - 1, y_zone(EY - 1), EX * EZ),
        (4, 1, third == 0, z_zone(0), EX * EY),
        (5, ZONES - 1, third == EZ - 1, z_zone(EZ - 1), EX * EY),
    )
    for k, shift, edge, zone_of, count in cases:
        moved = pltpu.roll(face(k).astype(F32), shift, 1)
        placed = dot(halo_refs[k][...], place_zones(zone_of, count))
        incoming_ref[FACE * k : FACE * (k + 1), :] = jnp.where(edge, placed, moved).astype(BF16)
    flux_ref[...] = dot(spread_ref[...], incoming_ref[...])


def fold(parts):
    row = lax.broadcasted_iota(jnp.int32, (8, TILE), 0)
    for half in (4, 2, 1):
        low = (row & half) == 0
        count = len(parts) // 2
        joined = []
        for n in range(count):
            a, b = parts[n], parts[n + count]
            x = jnp.where(low, a, b)
            y = jnp.where(low, b, a)
            if half == 4:
                joined.append(x + pltpu.roll(y, 4, 0))
            else:
                joined.append(x + jnp.where(low, pltpu.roll(y, 8 - half, 0), pltpu.roll(y, half, 0)))
        parts = joined
    return parts[0]


def apply_matrices(matrix_ref, values, out_ref):
    comps = [values[DOFS * c : DOFS * (c + 1)] for c in range(COMP)]

    def rows(block, carry):
        start = pl.multiple_of(block * (ROWS * DOFS), ROWS * DOFS)
        parts = [[None] * ROWS for _ in range(COMP)]
        for pair in range(ROWS // 2):
            piece = matrix_ref[:, pl.ds(start + pair * TILE, TILE)].T.astype(F32)
            for half in range(2):
                entry = piece[DOFS * half : DOFS * (half + 1)]
                for c in range(COMP):
                    product = entry * comps[c]
                    total = product[0:8]
                    for k in range(1, 8):
                        total = total + product[8 * k : 8 * k + 8]
                    parts[c][2 * pair + half] = total
        for c in range(COMP):
            out_ref[pl.ds(pl.multiple_of(c * DOFS + block * ROWS, ROWS), ROWS), :] = fold(parts[c])
        return carry

    lax.fori_loop(0, DOFS // ROWS, rows, 0)


def start_kernel(state_ref, owner_ref, pick_ref, flags_ref, u_ref, payload_ref, slot_ref, *send_refs):
    u = state_ref[...].T
    u_ref[...] = u
    write_faces(u.astype(BF16), pick_ref, flags_ref, payload_ref, send_refs)
    before = lax.broadcasted_iota(jnp.int32, (TILE, TILE), 0) < lax.broadcasted_iota(jnp.int32, (TILE, TILE), 1)
    before = jnp.where(before, 1.0, 0.0).astype(BF16)
    owners = lax.broadcasted_iota(jnp.int32, (128, TILE), 0)
    carry = jnp.zeros((128, 1), F32)
    for t in range(TILES):
        owner = owner_ref[:, TILE * t : TILE * (t + 1)]
        match = jnp.where(owners == owner, 1.0, 0.0)
        earlier = dot(match.astype(BF16), before) + carry
        rank = jnp.sum(earlier * match, axis=0, keepdims=True)
        slot_ref[:, TILE * t : TILE * (t + 1)] = owner * CAP + rank.astype(jnp.int32)
        carry = carry + jnp.sum(match, axis=1, keepdims=True)


def push_kernel(matrix_ref, u_ref, pushed_ref):
    work = u_ref[...].astype(BF16).astype(F32)
    apply_matrices(matrix_ref, work, pushed_ref)


def update(step, matrix_ref, u_ref, pushed_ref, low_ref, high_ref, payload_ref, halo_refs, spread_ref, incoming_ref, flux_ref, change_ref):
    @pl.when(step == 0)
    def _():
        incoming_flux(payload_ref, halo_refs, spread_ref, incoming_ref, flux_ref)

    lanes = pl.ds(pl.multiple_of(step * TILE, TILE), TILE)
    rhs = (pushed_ref[...] + flux_ref[:, lanes]).astype(BF16).astype(F32)
    apply_matrices(matrix_ref, rhs, change_ref)
    moved = u_ref[...] + change_ref[...]
    return lanes, jnp.minimum(jnp.maximum(moved, low_ref[...].T), high_ref[...].T)


def step_kernel(matrix_ref, u_ref, pushed_ref, low_ref, high_ref, payload_ref, *rest):
    halo_refs, (spread_ref, pick_ref, flags_ref), rest = rest[:6], rest[6:9], rest[9:]
    (next_ref, next_payload_ref), send_refs, rest = rest[:2], rest[2:8], rest[8:]
    incoming_ref, flux_ref, change_ref, work_ref = rest
    step = pl.program_id(0)
    lanes, u = update(
        step, matrix_ref, u_ref, pushed_ref, low_ref, high_ref, payload_ref, halo_refs, spread_ref, incoming_ref, flux_ref, change_ref
    )
    next_ref[...] = u
    work_ref[:, lanes] = u.astype(BF16)

    @pl.when(step == TILES - 1)
    def _():
        write_faces(work_ref[...], pick_ref, flags_ref, next_payload_ref, send_refs)


def last_kernel(matrix_ref, u_ref, pushed_ref, low_ref, high_ref, payload_ref, *rest):
    halo_refs, (spread_ref, slot_ref), rest = rest[:6], rest[6:8], rest[8:]
    outgoing_ref, incoming_ref, flux_ref, change_ref, work_ref = rest
    step = pl.program_id(0)
    lanes, u = update(
        step, matrix_ref, u_ref, pushed_ref, low_ref, high_ref, payload_ref, halo_refs, spread_ref, incoming_ref, flux_ref, change_ref
    )
    work_ref[:, lanes] = u.astype(BF16)

    @pl.when(step == TILES - 1)
    def _():
        chunk = 256
        slot = slot_ref[...]
        work = work_ref[...]

        def place(n, carry):
            first = pl.multiple_of(n * chunk, chunk)
            rows = lax.broadcasted_iota(jnp.int32, (chunk, ZONES), 0) + first
            match = jnp.where(rows == slot, 1.0, 0.0).astype(BF16)
            taken = lax.dot_general(match, work, (((1,), (1,)), ((), ())), preferred_element_type=F32)
            outgoing_ref[pl.ds(first, chunk), :] = taken.astype(BF16)
            return carry

        lax.fori_loop(0, outgoing_ref.shape[0] // chunk, place, 0)


def whole(shape):
    return pl.BlockSpec(shape, lambda t: (0,) * len(shape))


MATRIX = pl.BlockSpec((TILE, DOFS * DOFS), lambda t: (t, 0))
ROWMAJOR = pl.BlockSpec((TILE, WIDTH), lambda t: (t, 0))
COLUMNS = pl.BlockSpec((WIDTH, TILE), lambda t: (0, t))
SMEM = pl.BlockSpec(memory_space=pltpu.SMEM)
SEQUENTIAL = pltpu.CompilerParams(dimension_semantics=("arbitrary",))
TRANSPOSED = jax.ShapeDtypeStruct((WIDTH, ZONES), F32)
PAYLOAD = jax.ShapeDtypeStruct((6 * FACE, ZONES), BF16)
SEND_SHAPES = [jax.ShapeDtypeStruct(s, BF16) for s in SENDS]
UPDATE_SCRATCH = [
    pltpu.VMEM((6 * FACE, ZONES), BF16),
    pltpu.VMEM((WIDTH, ZONES), F32),
    pltpu.VMEM((WIDTH, TILE), F32),
    pltpu.VMEM((WIDTH, ZONES), BF16),
]


def begin(state, owner, pick, flags):
    return pl.pallas_call(
        start_kernel,
        in_specs=[pl.BlockSpec(memory_space=pltpu.VMEM)] * 3 + [SMEM],
        out_shape=[TRANSPOSED, PAYLOAD, jax.ShapeDtypeStruct((1, ZONES), jnp.int32)] + SEND_SHAPES,
        name="begin",
    )(state, owner, pick, flags)


def push(convection, u):
    return pl.pallas_call(
        push_kernel,
        grid=(TILES,),
        in_specs=[MATRIX, COLUMNS],
        out_specs=COLUMNS,
        out_shape=TRANSPOSED,
        compiler_params=SEQUENTIAL,
        name="push",
    )(convection, u)


UPDATE_SPECS = [MATRIX, COLUMNS, COLUMNS, ROWMAJOR, ROWMAJOR, whole((6 * FACE, ZONES))] + [whole(s) for s in SENDS]


def step_on(args, spread, pick, flags):
    return pl.pallas_call(
        step_kernel,
        grid=(TILES,),
        in_specs=UPDATE_SPECS + [whole((WIDTH, 6 * FACE)), whole((6 * FACE, WIDTH)), SMEM],
        out_specs=[COLUMNS, whole((6 * FACE, ZONES))] + [whole(s) for s in SENDS],
        out_shape=[TRANSPOSED, PAYLOAD] + SEND_SHAPES,
        scratch_shapes=UPDATE_SCRATCH,
        compiler_params=SEQUENTIAL,
        name="step_on",
    )(*args, spread, pick, flags)


def finish(args, spread, slot, slots):
    return pl.pallas_call(
        last_kernel,
        grid=(TILES,),
        in_specs=UPDATE_SPECS + [whole((WIDTH, 6 * FACE)), whole((1, ZONES))],
        out_specs=whole((slots, WIDTH)),
        out_shape=jax.ShapeDtypeStruct((slots, WIDTH), BF16),
        scratch_shapes=UPDATE_SCRATCH,
        compiler_params=SEQUENTIAL,
        name="finish",
    )(*args, spread, slot)


def exchange(sends):
    halos = []
    for k, send in enumerate(sends):
        axis = AXES[k // 2]
        count = lax.axis_size(axis)
        move = 1 if k % 2 == 0 else -1
        halos.append(lax.ppermute(send, axis, [(i, (i + move) % count) for i in range(count)]))
    return halos


def shards(state, convection, inverse_mass, face_coupling, lower_bound, upper_bound, new_owner):
    state = state.reshape(ZONES, WIDTH)
    convection = convection.reshape(ZONES, DOFS * DOFS)
    inverse_mass = inverse_mass.reshape(ZONES, DOFS * DOFS)
    lower_bound = lower_bound.reshape(ZONES, WIDTH)
    upper_bound = upper_bound.reshape(ZONES, WIDTH)
    owner = new_owner.reshape(1, ZONES)
    devices = lax.axis_size(AXES)
    identity = jnp.eye(COMP, dtype=BF16)
    blocks = face_coupling.reshape(6, 16, DOFS)
    spread = (blocks.transpose(2, 0, 1)[None, :, :, None, :] * identity[:, None, None, :, None]).reshape(WIDTH, 6 * FACE)
    pick = jnp.asarray(pick_table(), BF16)
    flags = []
    for axis in AXES:
        index = lax.axis_index(axis)
        flags += [index < lax.axis_size(axis) - 1, index > 0]
    flags = jnp.stack(flags).astype(jnp.int32)

    u, payload, slot, *sends = begin(state, owner, pick, flags)
    halos = exchange(sends)
    pushed = push(convection, u)
    args = (inverse_mass, u, pushed, lower_bound, upper_bound, payload, *halos)
    u, payload, *sends = step_on(args, spread, pick, flags)
    halos = exchange(sends)
    pushed = push(convection, u)
    args = (inverse_mass, u, pushed, lower_bound, upper_bound, payload, *halos)
    outgoing = finish(args, spread, slot, devices * CAP)
    arrived = lax.all_to_all(outgoing.reshape(devices, CAP, WIDTH), AXES, split_axis=0, concat_axis=0, tiled=True)
    return arrived.reshape(devices * CAP, WIDTH).astype(F32)


def solution(mesh):
    in_specs = (
        P("gx", "gy", "gz", None),
        P("gx", "gy", "gz", None),
        P("gx", "gy", "gz", None),
        P(),
        P("gx", "gy", "gz", None),
        P("gx", "gy", "gz", None),
        P(AXES, None, None),
    )
    out_specs = P(AXES, None)
    return jax.shard_map(shards, mesh=mesh, in_specs=in_specs, out_specs=out_specs, check_vma=False)
```

time: 210 us -> 111 us (0.53)
  local copies, waits for them, and re-layouts: 66.9 us -> 3.19 us
  Pallas kernels: 0 us -> 60.6 us
  matrix products: 53.3 us -> 0 us
  blocking collectives: 42.2 us -> 25.7 us
  starting transfers between devices: 33.7 us -> 18.5 us
  other arithmetic: 7.98 us -> 2.37 us
  waiting for transfers between devices: 3.55 us -> 0.03 us
    pallas_call x0 -> x5, Pallas kernels: none -> 60.6 us  [the longest x2 23.9 us: push(): pl.pallas_call(push_kernel, grid=(TILES,), in_specs=[MATRIX, COLUMNS], ou...]
    reshape x14 -> x0, local copies, waits for them, and re-layouts: 58.3 us -> none  [the longest x1 23.6 us: remap_step(): conv = convection.reshape(zones, DOFS, DOFS)]
    dot_general x21 -> x0, matrix products: 53.3 us -> none  [the longest x2 45.9 us: remap_step(): jnp.einsum('ecj,eij->eci', rhs, inverse, preferred_element_type=jnp.float32)]
    all_to_all x1, blocking collectives: 42.2 us -> 25.7 us  [shards(): lax.all_to_all(outgoing.reshape(devices, CAP, WIDTH), AXES, split_axis=0,...]
    ppermute x12, starting transfers between devices: 33.7 us -> 18.5 us  [exchange(): lax.ppermute(send, axis, [(i, (i + move) % count) for i in range(count)])]
    scatter x1 -> x0, local copies, waits for them, and re-layouts: 5.78 us -> none  [shards(): jnp.zeros((devices * capacity, width), jnp.float32).at[target].set(rows)]
    ppermute x12, waiting for transfers between devices: 3.55 us -> 0.03 us  [exchange(): lax.ppermute(send, axis, [(i, (i + move) % count) for i in range(count)])]
    min x1 -> x0, other arithmetic: 3.07 us -> none  [remap_step(): return jnp.minimum(jnp.maximum(moved, lower_bound), upper_bound)]
  transfers between devices with their start and end apart: 12 -> 12, of which waited for: 2 -> 0; matrix products, arithmetic and copies ran while one was open for 27% -> 2% of each run, Pallas kernels for 0% -> 22%
where the time goes in v1:
time: 111 us
  Pallas kernels  60.6 us (55%)
  blocking collectives  25.7 us (23%)
  starting transfers between devices  18.5 us (17%)
  local copies, waits for them, and re-layouts  3.19 us (3%)
  other arithmetic  2.37 us (2%)
    all_to_all x1, blocking collectives, shards(): lax.all_to_all(outgoing.reshape(devices, CAP, WIDTH), AXES, split_axis=0,...  25.7 us
    pallas_call x2, Pallas kernels, push(): pl.pallas_call(push_kernel, grid=(TILES,), in_specs=[MATRIX, COLUMNS], ou...  23.9 us
    ppermute x12, starting transfers between devices, exchange(): lax.ppermute(send, axis, [(i, (i + move) % count) for i in range(count)])  18.5 us
    pallas_call x1, Pallas kernels, finish(): pl.pallas_call(last_kernel, grid=(TILES,), in_specs=UPDATE_SPECS + [whole...  17.5 us
    pallas_call x1, Pallas kernels, step_on(): pl.pallas_call(step_kernel, grid=(TILES,), in_specs=UPDATE_SPECS + [whole...  15.9 us
    pallas_call x1, Pallas kernels, begin(): pl.pallas_call(start_kernel, in_specs=[pl.BlockSpec(memory_space=pltpu.VM...  3.29 us
  transfers between devices with their start and end apart: 12, of which 0 were waited for; matrix products, arithmetic and copies ran while one was open for 2% of the time, Pallas kernels for 22%

profile of v1, /device:TPU:1, one launch (start us, length us, event | category | flops | bytes accessed | tf_op | source)
XLA Modules:
  0.0 110.6 jit_solution(4001308338895811794)
XLA Ops:
  0.0 0.1 stack.27
  0.1 0.6 convert_element_type.16.flags_ref.rest_8_
  0.7 3.3 %begin.1 = (f32[256,1024]{1,0:T(8,128)}, bf16[384,1024]{1,0:T(8,128)(2,1)}, s32[1,1024]{1,0:T(1,128)}, bf16[64,256]{1,0:T(8,128)(2,1)}, bf16[64,256]{1,0:T(8,128...) custom-call(f32[1024,256]{1,0:T(8,128)} %bitcast.30, ...), custom_call_target="tpu_custom_call" | custom-call | tf_op jit(solution)/shard_map/begin/pallas_call | solution.py:248
  4.0 2.5 %collective-permute-start.2 = (bf16[64,128]{1,0:T(8,128)(2,1)}, bf16[64,128]{1,0:T(8,128)(2,1)S(1)}, u32[]{:S(2)}, u32[]{:S(2)}) collective-permute-start(bf16[64,128]{1,0:T(8,128)(2,1)} %get-tuple-element.26), channel_id=1, source_target_pairs={{0,8},{8,16},{16,24},{24,0},{1,9},{9,17},{17,25},{25,1},{2,10},{10... | collective-permute-start | bytes 49160 | tf_op jit(solution)/shard_map/ppermute | solution.py:303
  6.5 2.2 %collective-permute-start.3 = (bf16[64,128]{1,0:T(8,128)(2,1)}, bf16[64,128]{1,0:T(8,128)(2,1)S(1)}, u32[]{:S(2)}, u32[]{:S(2)}) collective-permute-start(bf16[64,128]{1,0:T(8,128)(2,1)} %get-tuple-element.27), channel_id=1, source_target_pairs={{0,24},{8,0},{16,8},{24,16},{1,25},{9,1},{17,9},{25,17},{2,26},{10... | collective-permute-start | bytes 49160 | tf_op jit(solution)/shard_map/ppermute | solution.py:303
  8.7 2.1 %collective-permute-start.4 = (bf16[64,128]{1,0:T(8,128)(2,1)}, bf16[64,128]{1,0:T(8,128)(2,1)S(1)}, u32[]{:S(2)}, u32[]{:S(2)}) collective-permute-start(bf16[64,128]{1,0:T(8,128)(2,1)} %get-tuple-element.28), channel_id=1, source_target_pairs={{0,1},{1,2},{2,3},{3,4},{4,5},{5,6},{6,7},{7,0},{8,9},{9,10},{10,1... | collective-permute-start | bytes 49160 | tf_op jit(solution)/shard_map/ppermute | solution.py:303
  10.9 0.0 collective-permute-start.5
  10.9 1.2 %collective-permute-start = (bf16[64,256]{1,0:T(8,128)(2,1)}, bf16[64,256]{1,0:T(8,128)(2,1)S(1)}, u32[]{:S(2)}, u32[]{:S(2)}) collective-permute-start(bf16[64,256]{1,0:T(8,128)(2,1)} %get-tuple-element.24), channel_id=1, source_target_pairs={{0,32},{32,64},{64,96},{96,0},{1,33},{33,65},{65,97},{97,1},{2,34}... | collective-permute-start | bytes 98312 | tf_op jit(solution)/shard_map/ppermute | solution.py:303
  12.1 0.8 copy.9
  12.9 0.0 collective-permute-done.2.rest_2_
  12.9 1.5 %collective-permute-start.1 = (bf16[64,256]{1,0:T(8,128)(2,1)}, bf16[64,256]{1,0:T(8,128)(2,1)S(1)}, u32[]{:S(2)}, u32[]{:S(2)}) collective-permute-start(bf16[64,256]{1,0:T(8,128)(2,1)} %get-tuple-element.25), channel_id=1, source_target_pairs={{0,96},{32,0},{64,32},{96,64},{1,97},{33,1},{65,33},{97,65},{2,98}... | collective-permute-start | bytes 98312 | tf_op jit(solution)/shard_map/ppermute | solution.py:303
  14.4 0.2 broadcast_multiply_fusion
  14.7 0.3 mul.20
  14.9 0.8 copy.10.rest_6_
  15.8 12.0 %push.2.pushed_ref = f32[256,1024]{1,0:T(8,128)} custom-call(bf16[1024,4096]{1,0:T(8,128)(2,1)} %bitcast.21, f32[256,1024]{1,0:T(8,128)} %get-tuple-element.22.u_ref), custom_call_target="tpu_custom_call" | custom-call | tf_op jit(solution)/shard_map/push/pallas_call | solution.py:257
  27.7 0.0 collective-permute-done.3.rest_3_
  27.7 0.0 collective-permute-done.4.rest_4_
  27.7 0.0 collective-permute-done.5.rest_5_
  27.8 0.0 collective-permute-done.rest_0_
  27.8 0.0 copy-start
  27.8 0.0 collective-permute-done.1.rest_1_
  27.8 0.5 copy-done.5
  28.3 0.0 copy-done.6
  28.3 0.0 copy-done.7
  28.3 0.0 copy-done
  28.4 0.0 copy-done.2
  28.4 15.9 %step_on.1 = (f32[256,1024]{1,0:T(8,128)}, bf16[384,1024]{1,0:T(8,128)(2,1)}, bf16[64,256]{1,0:T(8,128)(2,1)}, bf16[64,256]{1,0:T(8,128)(2,1)}, bf16[64,128]{1,0...) custom-call(bf16[1024,4096]{1,0:T(8,128)(2,1)} %bitcast.23, ...), custom_call_target="tpu_custom_call" | custom-call | tf_op jit(solution)/shard_map/step_on/pallas_call | solution.py:272
  44.3 0.1 collective-permute-start.8
  44.4 0.1 collective-permute-start.6
  44.5 2.7 %collective-permute-start.7 = (bf16[64,256]{1,0:T(8,128)(2,1)}, bf16[64,256]{1,0:T(8,128)(2,1)S(1)}, u32[]{:S(2)}, u32[]{:S(2)}) collective-permute-start(bf16[64,256]{1,0:T(8,128)(2,1)} %get-tuple-element.33), channel_id=1, source_target_pairs={{0,96},{32,0},{64,32},{96,64},{1,97},{33,1},{65,33},{97,65},{2,98}... | collective-permute-start | bytes 98312 | tf_op jit(solution)/shard_map/ppermute | solution.py:303
  47.2 2.6 %collective-permute-start.9 = (bf16[64,128]{1,0:T(8,128)(2,1)}, bf16[64,128]{1,0:T(8,128)(2,1)S(1)}, u32[]{:S(2)}, u32[]{:S(2)}) collective-permute-start(bf16[64,128]{1,0:T(8,128)(2,1)} %get-tuple-element.35), channel_id=1, source_target_pairs={{0,24},{8,0},{16,8},{24,16},{1,25},{9,1},{17,9},{25,17},{2,26},{10... | collective-permute-start | bytes 49160 | tf_op jit(solution)/shard_map/ppermute | solution.py:303
  49.8 3.4 %collective-permute-start.10 = (bf16[64,128]{1,0:T(8,128)(2,1)}, bf16[64,128]{1,0:T(8,128)(2,1)S(1)}, u32[]{:S(2)}, u32[]{:S(2)}) collective-permute-start(bf16[64,128]{1,0:T(8,128)(2,1)} %get-tuple-element.36), channel_id=1, source_target_pairs={{0,1},{1,2},{2,3},{3,4},{4,5},{5,6},{6,7},{7,0},{8,9},{9,10},{10,1... | collective-permute-start | bytes 49160 | tf_op jit(solution)/shard_map/ppermute | solution.py:303
  53.2 0.0 collective-permute-done.8.rest_2_
  53.2 0.0 collective-permute-start.11
  53.2 11.9 %push.3.pushed_ref = f32[256,1024]{1,0:T(8,128)} custom-call(bf16[1024,4096]{1,0:T(8,128)(2,1)} %bitcast.22, f32[256,1024]{1,0:T(8,128)} %get-tuple-element.30.u_ref), custom_call_target="tpu_custom_call" | custom-call | tf_op jit(solution)/shard_map/push/pallas_call | solution.py:257
  65.2 0.0 collective-permute-done.9.rest_3_
  65.2 0.0 collective-permute-done.10.rest_4_
  65.2 0.0 collective-permute-done.11.rest_5_
  65.2 0.0 collective-permute-done.6.rest_0_
  65.2 0.0 collective-permute-done.7.rest_1_
  65.2 0.5 copy-done.9
  65.8 0.0 copy-done.10
  65.8 0.0 copy-done.11
  65.8 0.0 copy-done.1
  65.8 0.0 copy-done.3
  65.8 17.5 %finish.1 = bf16[2048,256]{1,0:T(8,128)(2,1)} custom-call(bf16[1024,4096]{1,0:T(8,128)(2,1)} %bitcast.24, f32[256,1024]{1,0:T(8,128)} %get-tuple-element.30.u_ref, f32[256,1024]{1,0:T(8,128)} %push.3.pushed_ref, f32[1024,256]{1,0:T(8,128)} %bitcast.27, f32[1024,256]{1,0:T(8,128)} %bitcast.29, bf16[384,1024]{1,0:T(8,128)(2,1)} %get-tuple-element.31.payload_ref, ...), custom_call_target="tpu_custom_call" | custom-call | tf_op jit(solution)/shard_map/finish/pallas_call | solution.py:285
  83.3 25.7 %all_to_all.5 = bf16[128,16,256]{2,1,0:T(8,128)(2,1)S(1)} all-to-all(bf16[128,16,256]{2,1,0:T(8,128)(2,1)} %bitcast.25), channel_id=1, replica_groups=mesh['gx'=4,'gy'=4,'gz'=8] {'gx','gy','gz'}, dimensions={0} | all-to-all | bytes 2097152 | tf_op jit(solution)/shard_map/all_to_all | solution.py:334
  109.1 1.5 %bitcast_convert_fusion = f32[2048,256]{1,0:T(8,128)} fusion(bf16[128,16,256]{2,1,0:T(8,128)(2,1)S(1)} %all_to_all.5), kind=kLoop, calls=%fused_computation | loop fusion | flops 524288 | bytes 3145728 | tf_op jit(solution)/shard_map/convert_element_type | solution.py:335
  (14 shorter events, 0.0 us)
Async XLA Ops:
  4.0 8.9 %collective-permute-start.2 = (bf16[64,128]{1,0:T(8,128)(2,1)}, bf16[64,128]{1,0:T(8,128)(2,1)S(1)}, u32[]{:S(2)}, u32[]{:S(2)}) collective-permute-start(bf16[64,128]{1,0:T(8,128)(2,1)} %get-tuple-element.26), channel_id=1, source_target_pairs={{0,8},{8,16},{16,24},{24,0},{1,9},{9,17},{17,25},{25,1},{2,10},{10... | collective-permute-start | bytes 49160 | tf_op jit(solution)/shard_map/ppermute | solution.py:303
  6.5 21.2 %collective-permute-start.3 = (bf16[64,128]{1,0:T(8,128)(2,1)}, bf16[64,128]{1,0:T(8,128)(2,1)S(1)}, u32[]{:S(2)}, u32[]{:S(2)}) collective-permute-start(bf16[64,128]{1,0:T(8,128)(2,1)} %get-tuple-element.27), channel_id=1, source_target_pairs={{0,24},{8,0},{16,8},{24,16},{1,25},{9,1},{17,9},{25,17},{2,26},{10... | collective-permute-start | bytes 49160 | tf_op jit(solution)/shard_map/ppermute | solution.py:303
  8.7 19.0 %collective-permute-start.4 = (bf16[64,128]{1,0:T(8,128)(2,1)}, bf16[64,128]{1,0:T(8,128)(2,1)S(1)}, u32[]{:S(2)}, u32[]{:S(2)}) collective-permute-start(bf16[64,128]{1,0:T(8,128)(2,1)} %get-tuple-element.28), channel_id=1, source_target_pairs={{0,1},{1,2},{2,3},{3,4},{4,5},{5,6},{6,7},{7,0},{8,9},{9,10},{10,1... | collective-permute-start | bytes 49160 | tf_op jit(solution)/shard_map/ppermute | solution.py:303
  10.9 16.9 %collective-permute-start.5 = (bf16[64,128]{1,0:T(8,128)(2,1)}, bf16[64,128]{1,0:T(8,128)(2,1)S(1)}, u32[]{:S(2)}, u32[]{:S(2)}) collective-permute-start(bf16[64,128]{1,0:T(8,128)(2,1)} %get-tuple-element.29), channel_id=1, source_target_pairs={{0,7},{1,0},{2,1},{3,2},{4,3},{5,4},{6,5},{7,6},{8,15},{9,8},{10,9... | collective-permute-start | bytes 49160 | tf_op jit(solution)/shard_map/ppermute | solution.py:303
  10.9 16.9 %collective-permute-start = (bf16[64,256]{1,0:T(8,128)(2,1)}, bf16[64,256]{1,0:T(8,128)(2,1)S(1)}, u32[]{:S(2)}, u32[]{:S(2)}) collective-permute-start(bf16[64,256]{1,0:T(8,128)(2,1)} %get-tuple-element.24), channel_id=1, source_target_pairs={{0,32},{32,64},{64,96},{96,0},{1,33},{33,65},{65,97},{97,1},{2,34}... | collective-permute-start | bytes 98312 | tf_op jit(solution)/shard_map/ppermute | solution.py:303
  12.9 14.9 %copy-start.4 = (bf16[64,128]{1,0:T(8,128)(2,1)}, bf16[64,128]{1,0:T(8,128)(2,1)S(1)}, u32[]{:S(2)}) copy-start(bf16[64,128]{1,0:T(8,128)(2,1)S(1)} %collective-permute-done.2.rest_2_) | copy-start | bytes 49156
  12.9 14.9 %collective-permute-start.1 = (bf16[64,256]{1,0:T(8,128)(2,1)}, bf16[64,256]{1,0:T(8,128)(2,1)S(1)}, u32[]{:S(2)}, u32[]{:S(2)}) collective-permute-start(bf16[64,256]{1,0:T(8,128)(2,1)} %get-tuple-element.25), channel_id=1, source_target_pairs={{0,96},{32,0},{64,32},{96,64},{1,97},{33,1},{65,33},{97,65},{2,98}... | collective-permute-start | bytes 98312 | tf_op jit(solution)/shard_map/ppermute | solution.py:303
  27.7 0.6 copy-start.5
  27.7 0.6 copy-start.6
  27.7 0.6 copy-start.7
  27.8 0.6 copy-start
  27.8 0.6 copy-start.2
  44.3 8.8 %collective-permute-start.8 = (bf16[64,128]{1,0:T(8,128)(2,1)}, bf16[64,128]{1,0:T(8,128)(2,1)S(1)}, u32[]{:S(2)}, u32[]{:S(2)}) collective-permute-start(bf16[64,128]{1,0:T(8,128)(2,1)} %get-tuple-element.34), channel_id=1, source_target_pairs={{0,8},{8,16},{16,24},{24,0},{1,9},{9,17},{17,25},{25,1},{2,10},{10... | collective-permute-start | bytes 49160 | tf_op jit(solution)/shard_map/ppermute | solution.py:303
  44.4 20.8 %collective-permute-start.6 = (bf16[64,256]{1,0:T(8,128)(2,1)}, bf16[64,256]{1,0:T(8,128)(2,1)S(1)}, u32[]{:S(2)}, u32[]{:S(2)}) collective-permute-start(bf16[64,256]{1,0:T(8,128)(2,1)} %get-tuple-element.32), channel_id=1, source_target_pairs={{0,32},{32,64},{64,96},{96,0},{1,33},{33,65},{65,97},{97,1},{2,34}... | collective-permute-start | bytes 98312 | tf_op jit(solution)/shard_map/ppermute | solution.py:303
  44.5 20.7 %collective-permute-start.7 = (bf16[64,256]{1,0:T(8,128)(2,1)}, bf16[64,256]{1,0:T(8,128)(2,1)S(1)}, u32[]{:S(2)}, u32[]{:S(2)}) collective-permute-start(bf16[64,256]{1,0:T(8,128)(2,1)} %get-tuple-element.33), channel_id=1, source_target_pairs={{0,96},{32,0},{64,32},{96,64},{1,97},{33,1},{65,33},{97,65},{2,98}... | collective-permute-start | bytes 98312 | tf_op jit(solution)/shard_map/ppermute | solution.py:303
  47.2 18.0 %collective-permute-start.9 = (bf16[64,128]{1,0:T(8,128)(2,1)}, bf16[64,128]{1,0:T(8,128)(2,1)S(1)}, u32[]{:S(2)}, u32[]{:S(2)}) collective-permute-start(bf16[64,128]{1,0:T(8,128)(2,1)} %get-tuple-element.35), channel_id=1, source_target_pairs={{0,24},{8,0},{16,8},{24,16},{1,25},{9,1},{17,9},{25,17},{2,26},{10... | collective-permute-start | bytes 49160 | tf_op jit(solution)/shard_map/ppermute | solution.py:303
  49.8 15.4 %collective-permute-start.10 = (bf16[64,128]{1,0:T(8,128)(2,1)}, bf16[64,128]{1,0:T(8,128)(2,1)S(1)}, u32[]{:S(2)}, u32[]{:S(2)}) collective-permute-start(bf16[64,128]{1,0:T(8,128)(2,1)} %get-tuple-element.36), channel_id=1, source_target_pairs={{0,1},{1,2},{2,3},{3,4},{4,5},{5,6},{6,7},{7,0},{8,9},{9,10},{10,1... | collective-permute-start | bytes 49160 | tf_op jit(solution)/shard_map/ppermute | solution.py:303
  53.2 12.1 %copy-start.8 = (bf16[64,128]{1,0:T(8,128)(2,1)}, bf16[64,128]{1,0:T(8,128)(2,1)S(1)}, u32[]{:S(2)}) copy-start(bf16[64,128]{1,0:T(8,128)(2,1)S(1)} %collective-permute-done.8.rest_2_) | copy-start | bytes 49156
  53.2 12.0 %collective-permute-start.11 = (bf16[64,128]{1,0:T(8,128)(2,1)}, bf16[64,128]{1,0:T(8,128)(2,1)S(1)}, u32[]{:S(2)}, u32[]{:S(2)}) collective-permute-start(bf16[64,128]{1,0:T(8,128)(2,1)} %get-tuple-element.37), channel_id=1, source_target_pairs={{0,7},{1,0},{2,1},{3,2},{4,3},{5,4},{6,5},{7,6},{8,15},{9,8},{10,9... | collective-permute-start | bytes 49160 | tf_op jit(solution)/shard_map/ppermute | solution.py:303
  65.2 0.6 copy-start.9
  65.2 0.6 copy-start.10
  65.2 0.6 copy-start.11
  65.2 0.6 copy-start.1
  65.2 0.6 copy-start.3

commit v2 on v1

v2 whole, which is shorter than its diff:
```python
import jax
import jax.numpy as jnp
import numpy as np
from jax import lax
from jax.experimental import pallas as pl
from jax.experimental.pallas import tpu as pltpu
from jax.sharding import PartitionSpec as P

COMP = 4
DOFS = 64
STEPS = 2
WIDTH = COMP * DOFS
EX, EY, EZ = 4, 8, 32
ZONES = EX * EY * EZ
PLANE = EY * EZ
TILE = 128
TILES = ZONES // TILE
GROUP = 16
FACE = COMP * 16
CAP = 16
AXES = ("gx", "gy", "gz")
F32 = jnp.float32
BF16 = jnp.bfloat16
ORDER = np.arange(WIDTH).reshape(COMP, DOFS // 2, 2).transpose(1, 0, 2).reshape(WIDTH)


def pick_table():
    table = np.zeros((6, COMP, 16, COMP, 4, 4, 4), np.float32)
    for c in range(COMP):
        for f in range(16):
            p, q = f // 4, f % 4
            for side, level in ((0, 3), (1, 0)):
                table[0 + side, c, f, c, level, p, q] = 1
                table[2 + side, c, f, c, p, level, q] = 1
                table[4 + side, c, f, c, p, q, level] = 1
    return table.reshape(6 * FACE, WIDTH)[:, ORDER]


def expand_table():
    table = np.zeros((COMP, DOFS, WIDTH * 2), np.float32)
    for n, c in enumerate((0, 1, 2, 3, 1, 0, 3, 2)):
        table[c, :, DOFS * n : DOFS * (n + 1)] = np.eye(DOFS)
    return table.reshape(WIDTH, 2 * WIDTH)[ORDER]


def coupling_tables():
    rows = np.tile(np.eye(DOFS, dtype=np.float32), (COMP, 1))[ORDER]
    columns = np.zeros((6, 16, 6, COMP, 16), np.float32)
    for k in range(6):
        for f in range(16):
            columns[k, f, k, :, f] = 1
    return rows, columns.reshape(96, 6 * FACE)


def order_table():
    return np.eye(WIDTH, dtype=np.float32)[:, ORDER]


def dot(a, b):
    return jnp.dot(a, b, preferred_element_type=F32)


def select_zones(zone_of, count):
    column = lax.broadcasted_iota(jnp.int32, (1, 128), 1)
    wanted = jnp.where(column < count, zone_of(column), -1)
    zone = lax.broadcasted_iota(jnp.int32, (ZONES, 128), 0)
    return jnp.where(zone == wanted, 1.0, 0.0).astype(BF16)


def place_zones(zone_of, count):
    row = lax.broadcasted_iota(jnp.int32, (128, 1), 0)
    wanted = jnp.where(row < count, zone_of(row), -1)
    zone = lax.broadcasted_iota(jnp.int32, (128, ZONES), 1)
    return jnp.where(zone == wanted, 1.0, 0.0).astype(BF16)


def y_zone(level):
    return lambda n: (n // EZ) * PLANE + level * EZ + n % EZ


def z_zone(level):
    return lambda n: n * EZ + level


SENDS = ((64, 256), (64, 256), (64, 128), (64, 128), (64, 128), (64, 128))


def write_faces(work, pick, payload_ref, send_refs):
    payload = dot(pick, work).astype(BF16)
    payload_ref[...] = payload

    def face(k):
        return payload[FACE * k : FACE * (k + 1)]

    pieces = (
        face(0)[:, ZONES - PLANE :].astype(F32),
        face(1)[:, :PLANE].astype(F32),
        dot(face(2), select_zones(y_zone(EY - 1), EX * EZ)),
        dot(face(3), select_zones(y_zone(0), EX * EZ)),
        dot(face(4), select_zones(z_zone(EZ - 1), EX * EY)),
        dot(face(5), select_zones(z_zone(0), EX * EY)),
    )
    for k in range(6):
        index = lax.axis_index(AXES[k // 2])
        inner = index > 0 if k % 2 else index < lax.axis_size(AXES[k // 2]) - 1
        send_refs[k][...] = jnp.where(inner, pieces[k], 0.0).astype(BF16)


def incoming_flux(payload_ref, halo_refs, spread_ref, incoming_ref):
    def face(k):
        return payload_ref[FACE * k : FACE * (k + 1), :]

    incoming_ref[0:FACE, 0:PLANE] = halo_refs[0][...]
    incoming_ref[0:FACE, PLANE:ZONES] = payload_ref[0:FACE, 0 : ZONES - PLANE]
    incoming_ref[FACE : 2 * FACE, 0 : ZONES - PLANE] = payload_ref[FACE : 2 * FACE, PLANE:ZONES]
    incoming_ref[FACE : 2 * FACE, ZONES - PLANE : ZONES] = halo_refs[1][...]
    zone = lax.broadcasted_iota(jnp.int32, (FACE, ZONES), 1)
    third = zone % EZ
    second = zone // EZ % EY
    cases = (
        (2, EZ, second == 0, y_zone(0), EX * EZ),
        (3, ZONES - EZ, second == EY - 1, y_zone(EY - 1), EX * EZ),
        (4, 1, third == 0, z_zone(0), EX * EY),
        (5, ZONES - 1, third == EZ - 1, z_zone(EZ - 1), EX * EY),
    )
    for k, shift, edge, zone_of, count in cases:
        moved = pltpu.roll(face(k).astype(F32), shift, 1)
        placed = dot(halo_refs[k][...], place_zones(zone_of, count))
        incoming_ref[FACE * k : FACE * (k + 1), :] = jnp.where(edge, placed, moved).astype(BF16)
    return dot(spread_ref[...], incoming_ref[...])


def swap_blocks(parts, axis, block):
    size = parts[0].shape[axis]
    place = lax.broadcasted_iota(jnp.int32, parts[0].shape, axis) // block
    parts = list(parts)
    half = len(parts) // 2
    while half:
        low = (place & half) == 0
        for v in range(len(parts)):
            if v & half == 0:
                a, b = parts[v], parts[v + half]
                parts[v] = jnp.where(low, a, pltpu.roll(b, half * block, axis))
                parts[v + half] = jnp.where(low, pltpu.roll(a, size - half * block, axis), b)
        half //= 2
    return parts


def turned(rows):
    columns = rows.T
    parts = []
    for k in range(DOFS // 8):
        parts += swap_blocks([columns[DOFS * c + 8 * k : DOFS * c + 8 * k + 8] for c in range(COMP)], 0, 2)
    return parts


def tile(t):
    return pl.ds(pl.multiple_of(t * TILE, TILE), TILE)


def fetches(pairs, sems, first=0):
    return [pltpu.make_async_copy(source, target, sems.at[first + n]) for n, (source, target) in enumerate(pairs)]


def fetch_tile(source_ref, target_ref, sems, t):
    return pltpu.make_async_copy(source_ref.at[tile(t)], target_ref.at[tile(t)], sems.at[t])


def apply_matrices(wait, matrix_ref, values_ref, expand_ref, left_ref, product_ref, emit):
    def expand(t, carry):
        expanded = lax.dot_general(
            values_ref[:, pl.ds(pl.multiple_of(t * 2 * TILE, 2 * TILE), 2 * TILE)],
            expand_ref[...],
            (((0,), (0,)), ((), ())),
            preferred_element_type=F32,
        )
        for n in range(8):
            c, s = n // 2, n % 2
            source = c // 2 + (0 if c % 2 == s else 2)
            left_ref[pl.ds(t * 16 * TILE + n, 2 * TILE, stride=8), :] = expanded[:, TILE * source : TILE * (source + 1)]
        return carry

    lax.fori_loop(0, TILES // 2, expand, 0)
    zone = lax.broadcasted_iota(jnp.int32, (8, DOFS // 2 * GROUP), 1) % GROUP
    shape = (8 * GROUP, TILE)
    half = lax.broadcasted_iota(jnp.int32, shape, 0) % 2 == lax.broadcasted_iota(jnp.int32, shape, 1) // DOFS

    def apply(t, carry):
        wait(t)
        for g in range(TILE // GROUP):
            first = pl.multiple_of(t * TILE + GROUP * g, GROUP)
            left = jnp.where(half, left_ref[pl.ds(pl.multiple_of(8 * first, 8 * GROUP), 8 * GROUP), :], 0.0).astype(BF16)
            matrix = matrix_ref[pl.ds(first, GROUP), :]
            right = jnp.concatenate([matrix[:, TILE * m : TILE * (m + 1)] for m in range(DOFS // 2)], axis=0)
            product = lax.dot_general(left, right, (((1,), (1,)), ((), ())), preferred_element_type=F32)
            kept = product[0:8]
            for z in range(1, GROUP):
                kept = jnp.where(zone == z, product[8 * z : 8 * z + 8], kept)
            product_ref[8 * g : 8 * g + 8, :] = kept
        for q in range(4):
            parts = [product_ref[8 * g : 8 * g + 8, TILE * q : TILE * (q + 1)] for g in range(TILE // GROUP)]
            for n, part in enumerate(swap_blocks(parts, 1, GROUP)):
                emit(t, 8 * q + n, part)
        return carry

    lax.fori_loop(0, TILES, apply, 0)


def start_kernel(*refs):
    sources, (u_ref, work_ref, payload_ref, slot_ref, spread_ref), send_refs = refs[:6], refs[6:11], refs[11:17]
    targets, sems = refs[17:23], refs[23]
    state_ref, pick_ref, owner_ref, coupling_ref, rows_ref, columns_ref = targets
    copies = fetches(list(zip(sources, targets)), sems)
    for copy in copies:
        copy.start()
    copies[0].wait()
    for t in range(TILES):
        lanes = slice(TILE * t, TILE * (t + 1))
        for m, part in enumerate(turned(state_ref[lanes, :])):
            u_ref[8 * m : 8 * m + 8, lanes] = part
    work = u_ref[...].astype(BF16)
    work_ref[...] = work
    copies[1].wait()
    write_faces(work, pick_ref[...], payload_ref, send_refs)
    for copy in copies[2:]:
        copy.wait()
    before = lax.broadcasted_iota(jnp.int32, (TILE, TILE), 0) < lax.broadcasted_iota(jnp.int32, (TILE, TILE), 1)
    before = jnp.where(before, 1.0, 0.0).astype(BF16)
    owners = lax.broadcasted_iota(jnp.int32, (128, TILE), 0)
    carry = jnp.zeros((128, 1), F32)
    for t in range(TILES):
        owner = owner_ref[:, TILE * t : TILE * (t + 1)]
        match = jnp.where(owners == owner, 1.0, 0.0)
        earlier = dot(match.astype(BF16), before) + carry
        rank = jnp.sum(earlier * match, axis=0, keepdims=True)
        slot_ref[:, TILE * t : TILE * (t + 1)] = owner * CAP + rank.astype(jnp.int32)
        carry = carry + jnp.sum(match, axis=1, keepdims=True)
    entries = dot(rows_ref[...], coupling_ref[...])
    entries = dot(entries.astype(BF16), columns_ref[...])
    own = lax.broadcasted_iota(jnp.int32, entries.shape, 0) // 2 % COMP
    theirs = lax.broadcasted_iota(jnp.int32, entries.shape, 1) // 16 % COMP
    spread_ref[...] = jnp.where(own == theirs, entries, 0.0).astype(BF16)


def push_kernel(matrix_source, expand_source, work_ref, pushed_ref, *scratch):
    left_ref, product_ref, matrix_ref, expand_ref, sems = scratch
    (expanded,) = fetches([(expand_source, expand_ref)], sems, TILES)
    expanded.start()
    for t in range(TILES):
        fetch_tile(matrix_source, matrix_ref, sems, t).start()
    expanded.wait()

    def emit(t, m, part):
        pushed_ref[8 * m : 8 * m + 8, tile(t)] = part

    def wait(t):
        fetch_tile(matrix_source, matrix_ref, sems, t).wait()

    apply_matrices(wait, matrix_ref, work_ref, expand_ref, left_ref, product_ref, emit)


def update(sources, fields, halo_refs, next_ref, scratch):
    u_ref, pushed_ref, payload_ref, spread_ref = fields
    incoming_ref, rhs_ref, left_ref, product_ref, matrix_ref, expand_ref, sems = scratch[:7]
    lower_ref, upper_ref, low_ref, high_ref, table_ref = scratch[7:]
    expanded, low, high, table = fetches(
        [(sources[3], expand_ref), (sources[1], low_ref), (sources[2], high_ref), (sources[4], table_ref)], sems, TILES
    )
    for copy in (expanded, low, high):
        copy.start()
    for t in range(TILES):
        fetch_tile(sources[0], matrix_ref, sems, t).start()
    table.start()
    rhs_ref[...] = (pushed_ref[...] + incoming_flux(payload_ref, halo_refs, spread_ref, incoming_ref)).astype(BF16)
    low.wait()
    high.wait()

    def bounds(t, carry):
        for m, part in enumerate(turned(low_ref[tile(t), :])):
            lower_ref[8 * m : 8 * m + 8, tile(t)] = part
        for m, part in enumerate(turned(high_ref[tile(t), :])):
            upper_ref[8 * m : 8 * m + 8, tile(t)] = part
        return carry

    lax.fori_loop(0, TILES, bounds, 0)
    expanded.wait()

    def emit(t, m, part):
        rows = slice(8 * m, 8 * m + 8)
        moved = u_ref[rows, tile(t)] + part
        next_ref[rows, tile(t)] = jnp.minimum(jnp.maximum(moved, lower_ref[rows, tile(t)]), upper_ref[rows, tile(t)])

    def wait(t):
        fetch_tile(sources[0], matrix_ref, sems, t).wait()

    apply_matrices(wait, matrix_ref, rhs_ref, expand_ref, left_ref, product_ref, emit)
    table.wait()
    return table_ref[...]


def step_kernel(*refs):
    sources, fields, halo_refs, refs = refs[:5], refs[5:9], refs[9:15], refs[15:]
    (next_ref, work_ref, next_payload_ref), send_refs, scratch = refs[:3], refs[3:9], refs[9:]
    pick = update(sources, fields, halo_refs, next_ref, scratch)
    work = next_ref[...].astype(BF16)
    work_ref[...] = work
    write_faces(work, pick, next_payload_ref, send_refs)


def last_kernel(*refs):
    sources, fields, halo_refs, slot_ref, refs = refs[:5], refs[5:9], refs[9:15], refs[15], refs[16:]
    outgoing_ref, next_ref, scratch = refs[0], refs[1], refs[2:]
    order = update(sources, fields, halo_refs, next_ref, scratch)
    chunk = 256
    slot = slot_ref[...]
    work = dot(order, next_ref[...].astype(BF16)).astype(BF16)

    def place(n, carry):
        first = pl.multiple_of(n * chunk, chunk)
        rows = lax.broadcasted_iota(jnp.int32, (chunk, ZONES), 0) + first
        match = jnp.where(rows == slot, 1.0, 0.0).astype(BF16)
        taken = lax.dot_general(match, work, (((1,), (1,)), ((), ())), preferred_element_type=F32)
        outgoing_ref[pl.ds(first, chunk), :] = taken.astype(BF16)
        return carry

    lax.fori_loop(0, outgoing_ref.shape[0] // chunk, place, 0)


INNER = pl.BlockSpec(memory_space=pltpu.VMEM)
SEND_SHAPES = [jax.ShapeDtypeStruct(s, BF16) for s in SENDS]
STATE = pltpu.VMEM((WIDTH, ZONES), F32)
WORK = pltpu.VMEM((WIDTH, ZONES), BF16)
PAYLOAD = pltpu.VMEM((6 * FACE, ZONES), BF16)
APPLY_SCRATCH = [
    pltpu.VMEM((8 * ZONES, TILE), F32),
    pltpu.VMEM((TILE // GROUP * 8, DOFS // 2 * GROUP), F32),
    pltpu.VMEM((ZONES, DOFS * DOFS), BF16),
    pltpu.VMEM((WIDTH, 2 * WIDTH), BF16),
    pltpu.SemaphoreType.DMA((TILES + 4,)),
]
ROWMAJOR = pltpu.VMEM((ZONES, WIDTH), F32)
UPDATE_SCRATCH = [PAYLOAD, WORK, *APPLY_SCRATCH, STATE, STATE, ROWMAJOR, ROWMAJOR]


def call(kernel, name, sources, args, out_shape, scratch_shapes, limit):
    args = [pltpu.with_memory_space_constraint(a, pltpu.VMEM) for a in args]
    sources = [pltpu.with_memory_space_constraint(a, pltpu.HBM) for a in sources]
    return pl.pallas_call(
        kernel,
        in_specs=[pl.BlockSpec(memory_space=pltpu.HBM)] * len(sources) + [INNER] * len(args),
        out_shape=out_shape,
        scratch_shapes=scratch_shapes,
        compiler_params=pltpu.CompilerParams(vmem_limit_bytes=limit << 20),
        name=name,
    )(*sources, *args)


def exchange(sends):
    halos = []
    for k, send in enumerate(sends):
        axis = AXES[k // 2]
        count = lax.axis_size(axis)
        move = 1 if k % 2 == 0 else -1
        halos.append(lax.ppermute(send, axis, [(i, (i + move) % count) for i in range(count)]))
    return halos


def shards(state, convection, inverse_mass, face_coupling, lower_bound, upper_bound, new_owner):
    state = state.reshape(ZONES, WIDTH)
    convection = convection.reshape(ZONES, DOFS * DOFS)
    inverse_mass = inverse_mass.reshape(ZONES, DOFS * DOFS)
    lower_bound = lower_bound.reshape(ZONES, WIDTH)
    upper_bound = upper_bound.reshape(ZONES, WIDTH)
    owner = new_owner.reshape(1, ZONES)
    devices = lax.axis_size(AXES)
    pick, expand, order, rows, columns = [
        jnp.asarray(t, BF16) for t in (pick_table(), expand_table(), order_table(), *coupling_tables())
    ]
    slots = pltpu.VMEM((1, ZONES), jnp.int32)
    table = pltpu.VMEM((WIDTH, 6 * FACE), BF16)
    sources = (state, pick, owner, face_coupling.T, rows, columns)
    state, work, payload, slot, spread, *sends = call(
        start_kernel,
        "begin",
        sources,
        (),
        [STATE, WORK, PAYLOAD, slots, table] + SEND_SHAPES,
        [pltpu.VMEM(a.shape, a.dtype) for a in sources] + [pltpu.SemaphoreType.DMA((len(sources),))],
        8,
    )
    for step in range(STEPS):
        halos = exchange(sends)
        pushed = call(push_kernel, "push", (convection, expand), (work,), STATE, APPLY_SCRATCH, 16)
        sources = (inverse_mass, lower_bound, upper_bound, expand)
        fields = (state, pushed, payload, spread, *halos)
        if step < STEPS - 1:
            state, work, payload, *sends = call(
                step_kernel,
                "step_on",
                (*sources, pick),
                fields,
                [STATE, WORK, PAYLOAD] + SEND_SHAPES,
                [*UPDATE_SCRATCH, pltpu.VMEM(pick.shape, BF16)],
                24,
            )
    outgoing = call(
        last_kernel,
        "finish",
        (*sources, order),
        (*fields, slot),
        jax.ShapeDtypeStruct((devices * CAP, WIDTH), BF16),
        [STATE, *UPDATE_SCRATCH, pltpu.VMEM(order.shape, BF16)],
        24,
    )
    arrived = lax.all_to_all(outgoing.reshape(devices, CAP, WIDTH), AXES, split_axis=0, concat_axis=0, tiled=True)
    return arrived.reshape(devices * CAP, WIDTH).astype(F32)


def solution(mesh):
    in_specs = (
        P("gx", "gy", "gz", None),
        P("gx", "gy", "gz", None),
        P("gx", "gy", "gz", None),
        P(),
        P("gx", "gy", "gz", None),
        P("gx", "gy", "gz", None),
        P(AXES, None, None),
    )
    out_specs = P(AXES, None)
    return jax.shard_map(shards, mesh=mesh, in_specs=in_specs, out_specs=out_specs, check_vma=False)
```

time: 111 us -> 86.9 us (0.78)
  Pallas kernels: 60.6 us -> 41.7 us
  local copies, waits for them, and re-layouts: 3.19 us -> 0 us
    pallas_call x5, Pallas kernels: 60.6 us -> 41.7 us  [call(): pl.pallas_call(kernel, in_specs=[pl.BlockSpec(memory_space=pltpu.HBM)] *...]
    unnamed x25 -> x0, local copies, waits for them, and re-layouts: 2 us -> none
  transfers between devices with their start and end apart: 12 -> 12, of which waited for: 0 -> 0; matrix products, arithmetic and copies ran while one was open for 2% -> 0% of each run, Pallas kernels for 22% -> 18%
where the time goes in v2:
time: 86.9 us; the launch traced here: 86.7 us
  Pallas kernels  41.7 us (48%)
  blocking collectives  24.9 us (29%)
  starting transfers between devices  18.4 us (21%)
  other arithmetic  1.55 us (2%)
    pallas_call x5, Pallas kernels, call(): pl.pallas_call(kernel, in_specs=[pl.BlockSpec(memory_space=pltpu.HBM)] *...  41.7 us
    all_to_all x1, blocking collectives, shards(): lax.all_to_all(outgoing.reshape(devices, CAP, WIDTH), AXES, split_axis=0,...  24.9 us
    ppermute x12, starting transfers between devices, exchange(): lax.ppermute(send, axis, [(i, (i + move) % count) for i in range(count)])  18.4 us
  transfers between devices with their start and end apart: 12, of which 0 were waited for; matrix products, arithmetic and copies ran while one was open for 0% of the time, Pallas kernels for 18%

profile of v2, /device:TPU:1, one launch (start us, length us, event | category | flops | bytes accessed | tf_op | source)
XLA Modules:
  0.0 86.7 jit_solution(12795400188545525639)
XLA Ops:
  0.0 2.7 %begin.1 = (f32[256,1024]{1,0:T(8,128)S(1)}, bf16[256,1024]{1,0:T(8,128)(2,1)S(1)}, bf16[384,1024]{1,0:T(8,128)(2,1)S(1)}, s32[1,1024]{1,0:T(1,128)S(1)}, bf16[2...) custom-call(f32[1024,256]{1,0:T(8,128)} %bitcast.20, ...), custom_call_target="tpu_custom_call" | custom-call | tf_op jit(solution)/shard_map/begin/pallas_call | solution.py:348
  2.7 2.5 %collective-permute-start.2 = (bf16[64,128]{1,0:T(8,128)(2,1)S(1)}, bf16[64,128]{1,0:T(8,128)(2,1)S(1)}, u32[]{:S(2)}, u32[]{:S(2)}) collective-permute-start(bf16[64,128]{1,0:T(8,128)(2,1)S(1)} %get-tuple-element.31), channel_id=1, source_target_pairs={{0,8},{8,16},{16,24},{24,0},{1,9},{9,17},{17,25},{25,1},{2,10},{10... | collective-permute-start | bytes 49160 | tf_op jit(solution)/shard_map/ppermute | solution.py:364
  5.3 1.2 %collective-permute-start = (bf16[64,256]{1,0:T(8,128)(2,1)S(1)}, bf16[64,256]{1,0:T(8,128)(2,1)S(1)}, u32[]{:S(2)}, u32[]{:S(2)}) collective-permute-start(bf16[64,256]{1,0:T(8,128)(2,1)S(1)} %get-tuple-element.29), channel_id=1, source_target_pairs={{0,32},{32,64},{64,96},{96,0},{1,33},{33,65},{65,97},{97,1},{2,34}... | collective-permute-start | bytes 98312 | tf_op jit(solution)/shard_map/ppermute | solution.py:364
  6.5 1.5 %collective-permute-start.1 = (bf16[64,256]{1,0:T(8,128)(2,1)S(1)}, bf16[64,256]{1,0:T(8,128)(2,1)S(1)}, u32[]{:S(2)}, u32[]{:S(2)}) collective-permute-start(bf16[64,256]{1,0:T(8,128)(2,1)S(1)} %get-tuple-element.30), channel_id=1, source_target_pairs={{0,96},{32,0},{64,32},{96,64},{1,97},{33,1},{65,33},{97,65},{2,98}... | collective-permute-start | bytes 98312 | tf_op jit(solution)/shard_map/ppermute | solution.py:364
  7.9 2.2 %collective-permute-start.3 = (bf16[64,128]{1,0:T(8,128)(2,1)S(1)}, bf16[64,128]{1,0:T(8,128)(2,1)S(1)}, u32[]{:S(2)}, u32[]{:S(2)}) collective-permute-start(bf16[64,128]{1,0:T(8,128)(2,1)S(1)} %get-tuple-element.32), channel_id=1, source_target_pairs={{0,24},{8,0},{16,8},{24,16},{1,25},{9,1},{17,9},{25,17},{2,26},{10... | collective-permute-start | bytes 49160 | tf_op jit(solution)/shard_map/ppermute | solution.py:364
  10.1 2.7 %collective-permute-start.4 = (bf16[64,128]{1,0:T(8,128)(2,1)S(1)}, bf16[64,128]{1,0:T(8,128)(2,1)S(1)}, u32[]{:S(2)}, u32[]{:S(2)}) collective-permute-start(bf16[64,128]{1,0:T(8,128)(2,1)S(1)} %get-tuple-element.33), channel_id=1, source_target_pairs={{0,1},{1,2},{2,3},{3,4},{4,5},{5,6},{6,7},{7,0},{8,9},{9,10},{10,1... | collective-permute-start | bytes 49160 | tf_op jit(solution)/shard_map/ppermute | solution.py:364
  12.8 0.0 collective-permute-done.2.refs_11_
  12.8 0.0 collective-permute-start.5
  12.8 7.8 %push.2.refs_6_ = f32[256,1024]{1,0:T(8,128)S(1)} custom-call(bf16[1024,4096]{1,0:T(8,128)(2,1)} %bitcast.12, bf16[256,512]{1,0:T(8,128)(2,1)} %constant.11.clone.expand_source.refs_3_, bf16[256,1024]{1,0:T(8,128)(2,1)S(1)} %get-tuple-element.26.work_ref), custom_call_target="tpu_custom_call" | custom-call | tf_op jit(solution)/shard_map/push/pallas_call | solution.py:348
  20.6 0.0 collective-permute-done.3.refs_12_
  20.6 0.0 collective-permute-done.4.refs_13_
  20.6 0.0 collective-permute-done.5.refs_14_
  20.6 0.0 collective-permute-done.refs_9_
  20.7 0.0 collective-permute-done.1.refs_10_
  20.7 10.5 %step_on.1 = (f32[256,1024]{1,0:T(8,128)S(1)}, bf16[256,1024]{1,0:T(8,128)(2,1)S(1)}, bf16[384,1024]{1,0:T(8,128)(2,1)S(1)}, bf16[64,256]{1,0:T(8,128)(2,1)S(1)}...) custom-call(bf16[1024,4096]{1,0:T(8,128)(2,1)} %bitcast.14, ...), custom_call_target="tpu_custom_call" | custom-call | tf_op jit(solution)/shard_map/step_on/pallas_call | solution.py:348
  31.2 0.1 collective-permute-start.8
  31.3 0.1 collective-permute-start.6
  31.4 2.7 %collective-permute-start.7 = (bf16[64,256]{1,0:T(8,128)(2,1)S(1)}, bf16[64,256]{1,0:T(8,128)(2,1)S(1)}, u32[]{:S(2)}, u32[]{:S(2)}) collective-permute-start(bf16[64,256]{1,0:T(8,128)(2,1)S(1)} %get-tuple-element.39), channel_id=1, source_target_pairs={{0,96},{32,0},{64,32},{96,64},{1,97},{33,1},{65,33},{97,65},{2,98}... | collective-permute-start | bytes 98312 | tf_op jit(solution)/shard_map/ppermute | solution.py:364
  34.0 2.6 %collective-permute-start.9 = (bf16[64,128]{1,0:T(8,128)(2,1)S(1)}, bf16[64,128]{1,0:T(8,128)(2,1)S(1)}, u32[]{:S(2)}, u32[]{:S(2)}) collective-permute-start(bf16[64,128]{1,0:T(8,128)(2,1)S(1)} %get-tuple-element.41), channel_id=1, source_target_pairs={{0,24},{8,0},{16,8},{24,16},{1,25},{9,1},{17,9},{25,17},{2,26},{10... | collective-permute-start | bytes 49160 | tf_op jit(solution)/shard_map/ppermute | solution.py:364
  36.6 2.9 %collective-permute-start.10 = (bf16[64,128]{1,0:T(8,128)(2,1)S(1)}, bf16[64,128]{1,0:T(8,128)(2,1)S(1)}, u32[]{:S(2)}, u32[]{:S(2)}) collective-permute-start(bf16[64,128]{1,0:T(8,128)(2,1)S(1)} %get-tuple-element.42), channel_id=1, source_target_pairs={{0,1},{1,2},{2,3},{3,4},{4,5},{5,6},{6,7},{7,0},{8,9},{9,10},{10,1... | collective-permute-start | bytes 49160 | tf_op jit(solution)/shard_map/ppermute | solution.py:364
  39.5 0.0 collective-permute-done.8.refs_11_
  39.5 0.0 collective-permute-start.11
  39.5 7.8 %push.3.refs_6_ = f32[256,1024]{1,0:T(8,128)S(1)} custom-call(bf16[1024,4096]{1,0:T(8,128)(2,1)} %bitcast.13, bf16[256,512]{1,0:T(8,128)(2,1)} %constant.11.clone.expand_source.refs_3_, bf16[256,1024]{1,0:T(8,128)(2,1)S(1)} %get-tuple-element.36.work_ref), custom_call_target="tpu_custom_call" | custom-call | tf_op jit(solution)/shard_map/push/pallas_call | solution.py:348
  47.3 0.0 collective-permute-done.9.refs_12_
  47.3 0.0 collective-permute-done.10.refs_13_
  47.3 0.0 collective-permute-done.11.refs_14_
  47.3 0.0 collective-permute-done.6.refs_9_
  47.3 0.0 collective-permute-done.7.refs_10_
  47.3 12.9 %finish.1 = bf16[2048,256]{1,0:T(8,128)(2,1)S(1)} custom-call(bf16[1024,4096]{1,0:T(8,128)(2,1)} %bitcast.15, f32[1024,256]{1,0:T(8,128)} %bitcast.17, f32[1024,256]{1,0:T(8,128)} %bitcast.19, bf16[256,512]{1,0:T(8,128)(2,1)} %constant.11.clone.expand_source.refs_3_, bf16[256,256]{1,0:T(8,128)(2,1)} %constant.12.clone.refs_4_, ...), custom_call_target="tpu_custom_call" | custom-call | tf_op jit(solution)/shard_map/finish/pallas_call | solution.py:348
  60.3 24.9 %all_to_all.5 = bf16[128,16,256]{2,1,0:T(8,128)(2,1)S(1)} all-to-all(bf16[128,16,256]{2,1,0:T(8,128)(2,1)S(1)} %bitcast.11), channel_id=1, replica_groups=mesh['gx'=4,'gy'=4,'gz'=8] {'gx','gy','gz'}, dimensions={0} | all-to-all | bytes 2097152 | tf_op jit(solution)/shard_map/all_to_all | solution.py:415
  85.2 1.5 %bitcast_convert_fusion = f32[2048,256]{1,0:T(8,128)} fusion(bf16[128,16,256]{2,1,0:T(8,128)(2,1)S(1)} %all_to_all.5), kind=kLoop, calls=%fused_computation | loop fusion | flops 524288 | bytes 3145728 | tf_op jit(solution)/shard_map/convert_element_type | solution.py:416
Async XLA Ops:
  2.7 10.1 %collective-permute-start.2 = (bf16[64,128]{1,0:T(8,128)(2,1)S(1)}, bf16[64,128]{1,0:T(8,128)(2,1)S(1)}, u32[]{:S(2)}, u32[]{:S(2)}) collective-permute-start(bf16[64,128]{1,0:T(8,128)(2,1)S(1)} %get-tuple-element.31), channel_id=1, source_target_pairs={{0,8},{8,16},{16,24},{24,0},{1,9},{9,17},{17,25},{25,1},{2,10},{10... | collective-permute-start | bytes 49160 | tf_op jit(solution)/shard_map/ppermute | solution.py:364
  5.3 15.4 %collective-permute-start = (bf16[64,256]{1,0:T(8,128)(2,1)S(1)}, bf16[64,256]{1,0:T(8,128)(2,1)S(1)}, u32[]{:S(2)}, u32[]{:S(2)}) collective-permute-start(bf16[64,256]{1,0:T(8,128)(2,1)S(1)} %get-tuple-element.29), channel_id=1, source_target_pairs={{0,32},{32,64},{64,96},{96,0},{1,33},{33,65},{65,97},{97,1},{2,34}... | collective-permute-start | bytes 98312 | tf_op jit(solution)/shard_map/ppermute | solution.py:364
  6.5 14.2 %collective-permute-start.1 = (bf16[64,256]{1,0:T(8,128)(2,1)S(1)}, bf16[64,256]{1,0:T(8,128)(2,1)S(1)}, u32[]{:S(2)}, u32[]{:S(2)}) collective-permute-start(bf16[64,256]{1,0:T(8,128)(2,1)S(1)} %get-tuple-element.30), channel_id=1, source_target_pairs={{0,96},{32,0},{64,32},{96,64},{1,97},{33,1},{65,33},{97,65},{2,98}... | collective-permute-start | bytes 98312 | tf_op jit(solution)/shard_map/ppermute | solution.py:364
  7.9 12.7 %collective-permute-start.3 = (bf16[64,128]{1,0:T(8,128)(2,1)S(1)}, bf16[64,128]{1,0:T(8,128)(2,1)S(1)}, u32[]{:S(2)}, u32[]{:S(2)}) collective-permute-start(bf16[64,128]{1,0:T(8,128)(2,1)S(1)} %get-tuple-element.32), channel_id=1, source_target_pairs={{0,24},{8,0},{16,8},{24,16},{1,25},{9,1},{17,9},{25,17},{2,26},{10... | collective-permute-start | bytes 49160 | tf_op jit(solution)/shard_map/ppermute | solution.py:364
  10.1 10.5 %collective-permute-start.4 = (bf16[64,128]{1,0:T(8,128)(2,1)S(1)}, bf16[64,128]{1,0:T(8,128)(2,1)S(1)}, u32[]{:S(2)}, u32[]{:S(2)}) collective-permute-start(bf16[64,128]{1,0:T(8,128)(2,1)S(1)} %get-tuple-element.33), channel_id=1, source_target_pairs={{0,1},{1,2},{2,3},{3,4},{4,5},{5,6},{6,7},{7,0},{8,9},{9,10},{10,1... | collective-permute-start | bytes 49160 | tf_op jit(solution)/shard_map/ppermute | solution.py:364
  12.8 7.8 %collective-permute-start.5 = (bf16[64,128]{1,0:T(8,128)(2,1)S(1)}, bf16[64,128]{1,0:T(8,128)(2,1)S(1)}, u32[]{:S(2)}, u32[]{:S(2)}) collective-permute-start(bf16[64,128]{1,0:T(8,128)(2,1)S(1)} %get-tuple-element.34), channel_id=1, source_target_pairs={{0,7},{1,0},{2,1},{3,2},{4,3},{5,4},{6,5},{7,6},{8,15},{9,8},{10,9... | collective-permute-start | bytes 49160 | tf_op jit(solution)/shard_map/ppermute | solution.py:364
  31.2 8.3 %collective-permute-start.8 = (bf16[64,128]{1,0:T(8,128)(2,1)S(1)}, bf16[64,128]{1,0:T(8,128)(2,1)S(1)}, u32[]{:S(2)}, u32[]{:S(2)}) collective-permute-start(bf16[64,128]{1,0:T(8,128)(2,1)S(1)} %get-tuple-element.40), channel_id=1, source_target_pairs={{0,8},{8,16},{16,24},{24,0},{1,9},{9,17},{17,25},{25,1},{2,10},{10... | collective-permute-start | bytes 49160 | tf_op jit(solution)/shard_map/ppermute | solution.py:364
  31.3 16.0 %collective-permute-start.6 = (bf16[64,256]{1,0:T(8,128)(2,1)S(1)}, bf16[64,256]{1,0:T(8,128)(2,1)S(1)}, u32[]{:S(2)}, u32[]{:S(2)}) collective-permute-start(bf16[64,256]{1,0:T(8,128)(2,1)S(1)} %get-tuple-element.38), channel_id=1, source_target_pairs={{0,32},{32,64},{64,96},{96,0},{1,33},{33,65},{65,97},{97,1},{2,34}... | collective-permute-start | bytes 98312 | tf_op jit(solution)/shard_map/ppermute | solution.py:364
  31.4 16.0 %collective-permute-start.7 = (bf16[64,256]{1,0:T(8,128)(2,1)S(1)}, bf16[64,256]{1,0:T(8,128)(2,1)S(1)}, u32[]{:S(2)}, u32[]{:S(2)}) collective-permute-start(bf16[64,256]{1,0:T(8,128)(2,1)S(1)} %get-tuple-element.39), channel_id=1, source_target_pairs={{0,96},{32,0},{64,32},{96,64},{1,97},{33,1},{65,33},{97,65},{2,98}... | collective-permute-start | bytes 98312 | tf_op jit(solution)/shard_map/ppermute | solution.py:364
  34.0 13.3 %collective-permute-start.9 = (bf16[64,128]{1,0:T(8,128)(2,1)S(1)}, bf16[64,128]{1,0:T(8,128)(2,1)S(1)}, u32[]{:S(2)}, u32[]{:S(2)}) collective-permute-start(bf16[64,128]{1,0:T(8,128)(2,1)S(1)} %get-tuple-element.41), channel_id=1, source_target_pairs={{0,24},{8,0},{16,8},{24,16},{1,25},{9,1},{17,9},{25,17},{2,26},{10... | collective-permute-start | bytes 49160 | tf_op jit(solution)/shard_map/ppermute | solution.py:364
  36.6 10.7 %collective-permute-start.10 = (bf16[64,128]{1,0:T(8,128)(2,1)S(1)}, bf16[64,128]{1,0:T(8,128)(2,1)S(1)}, u32[]{:S(2)}, u32[]{:S(2)}) collective-permute-start(bf16[64,128]{1,0:T(8,128)(2,1)S(1)} %get-tuple-element.42), channel_id=1, source_target_pairs={{0,1},{1,2},{2,3},{3,4},{4,5},{5,6},{6,7},{7,0},{8,9},{9,10},{10,1... | collective-permute-start | bytes 49160 | tf_op jit(solution)/shard_map/ppermute | solution.py:364
  39.5 7.8 %collective-permute-start.11 = (bf16[64,128]{1,0:T(8,128)(2,1)S(1)}, bf16[64,128]{1,0:T(8,128)(2,1)S(1)}, u32[]{:S(2)}, u32[]{:S(2)}) collective-permute-start(bf16[64,128]{1,0:T(8,128)(2,1)S(1)} %get-tuple-element.43), channel_id=1, source_target_pairs={{0,7},{1,0},{2,1},{3,2},{4,3},{5,4},{6,5},{7,6},{8,15},{9,8},{10,9... | collective-permute-start | bytes 49160 | tf_op jit(solution)/shard_map/ppermute | solution.py:364

commit v3 on v2

--- a/solution.py
+++ b/solution.py
@@ -166,44 +166,58 @@
     return pltpu.make_async_copy(source_ref.at[tile(t)], target_ref.at[tile(t)], sems.at[t])
 
 
-def apply_matrices(wait, matrix_ref, values_ref, expand_ref, left_ref, product_ref, emit):
-    def expand(t, carry):
+def apply_matrices(wait, prepare, matrix_ref, values_ref, expand_ref, left_refs, product_refs, emit):
+    zone = lax.broadcasted_iota(jnp.int32, (8, DOFS // 2 * GROUP), 1) % GROUP
+    shape = (8 * GROUP, TILE)
+    half = lax.broadcasted_iota(jnp.int32, shape, 0) % 2 == lax.broadcasted_iota(jnp.int32, shape, 1) // DOFS
+
+    def expand(t, left_ref):
         expanded = lax.dot_general(
-            values_ref[:, pl.ds(pl.multiple_of(t * 2 * TILE, 2 * TILE), 2 * TILE)],
-            expand_ref[...],
-            (((0,), (0,)), ((), ())),
-            preferred_element_type=F32,
+            values_ref[:, tile(t)], expand_ref[...], (((0,), (0,)), ((), ())), preferred_element_type=F32
         )
         for n in range(8):
             c, s = n // 2, n % 2
             source = c // 2 + (0 if c % 2 == s else 2)
-            left_ref[pl.ds(t * 16 * TILE + n, 2 * TILE, stride=8), :] = expanded[:, TILE * source : TILE * (source + 1)]
-        return carry
-
-    lax.fori_loop(0, TILES // 2, expand, 0)
-    zone = lax.broadcasted_iota(jnp.int32, (8, DOFS // 2 * GROUP), 1) % GROUP
-    shape = (8 * GROUP, TILE)
-    half = lax.broadcasted_iota(jnp.int32, shape, 0) % 2 == lax.broadcasted_iota(jnp.int32, shape, 1) // DOFS
-
-    def apply(t, carry):
-        wait(t)
+            left_ref[pl.ds(n, TILE, stride=8), :] = expanded[:, TILE * source : TILE * (source + 1)]
+
+    def multiply(t, left_ref, product_ref):
         for g in range(TILE // GROUP):
-            first = pl.multiple_of(t * TILE + GROUP * g, GROUP)
-            left = jnp.where(half, left_ref[pl.ds(pl.multiple_of(8 * first, 8 * GROUP), 8 * GROUP), :], 0.0).astype(BF16)
-            matrix = matrix_ref[pl.ds(first, GROUP), :]
+            left = jnp.where(half, left_ref[8 * GROUP * g : 8 * GROUP * (g + 1), :], 0.0).astype(BF16)
+            matrix = matrix_ref[pl.ds(pl.multiple_of(t * TILE + GROUP * g, GROUP), GROUP), :]
             right = jnp.concatenate([matrix[:, TILE * m : TILE * (m + 1)] for m in range(DOFS // 2)], axis=0)
             product = lax.dot_general(left, right, (((1,), (1,)), ((), ())), preferred_element_type=F32)
             kept = product[0:8]
             for z in range(1, GROUP):
                 kept = jnp.where(zone == z, product[8 * z : 8 * z + 8], kept)
             product_ref[8 * g : 8 * g + 8, :] = kept
+
+    def settle(t, slot):
+        product_ref = product_refs[slot]
         for q in range(4):
             parts = [product_ref[8 * g : 8 * g + 8, TILE * q : TILE * (q + 1)] for g in range(TILE // GROUP)]
             for n, part in enumerate(swap_blocks(parts, 1, GROUP)):
-                emit(t, 8 * q + n, part)
+                emit(t, slot, 8 * q + n, part)
+
+    (even_left, odd_left), (even_product, odd_product) = left_refs, product_refs
+    expand(0, even_left)
+    odd_product[...] = jnp.zeros_like(odd_product)
+
+    def pair(n, carry):
+        t = 2 * n
+        wait(t)
+        wait(t + 1)
+        settle(jnp.maximum(t - 1, 0), 1)
+        prepare(t, 0)
+        expand(t + 1, odd_left)
+        multiply(t, even_left, even_product)
+        settle(t, 0)
+        prepare(t + 1, 1)
+        expand(jnp.minimum(t + 2, TILES - 1), even_left)
+        multiply(t + 1, odd_left, odd_product)
         return carry
 
-    lax.fori_loop(0, TILES, apply, 0)
+    lax.fori_loop(0, TILES // 2, pair, 0)
+    settle(TILES - 1, 1)
 
 
 def start_kernel(*refs):
@@ -243,26 +257,27 @@
 
 
 def push_kernel(matrix_source, expand_source, work_ref, pushed_ref, *scratch):
-    left_ref, product_ref, matrix_ref, expand_ref, sems = scratch
+    left_refs, product_refs, (matrix_ref, expand_ref, sems) = scratch[0:2], scratch[2:4], scratch[4:7]
     (expanded,) = fetches([(expand_source, expand_ref)], sems, TILES)
     expanded.start()
     for t in range(TILES):
         fetch_tile(matrix_source, matrix_ref, sems, t).start()
     expanded.wait()
 
-    def emit(t, m, part):
+    def emit(t, slot, m, part):
         pushed_ref[8 * m : 8 * m + 8, tile(t)] = part
 
     def wait(t):
         fetch_tile(matrix_source, matrix_ref, sems, t).wait()
 
-    apply_matrices(wait, matrix_ref, work_ref, expand_ref, left_ref, product_ref, emit)
+    apply_matrices(wait, lambda t, slot: None, matrix_ref, work_ref, expand_ref, left_refs, product_refs, emit)
 
 
 def update(sources, fields, halo_refs, next_ref, scratch):
     u_ref, pushed_ref, payload_ref, spread_ref = fields
-    incoming_ref, rhs_ref, left_ref, product_ref, matrix_ref, expand_ref, sems = scratch[:7]
-    lower_ref, upper_ref, low_ref, high_ref, table_ref = scratch[7:]
+    (incoming_ref, rhs_ref), left_refs, product_refs = scratch[0:2], scratch[2:4], scratch[4:6]
+    (matrix_ref, expand_ref, sems), lower_refs, upper_refs = scratch[6:9], scratch[9:11], scratch[11:13]
+    low_ref, high_ref, table_ref = scratch[13:]
     expanded, low, high, table = fetches(
         [(sources[3], expand_ref), (sources[1], low_ref), (sources[2], high_ref), (sources[4], table_ref)], sems, TILES
     )
@@ -274,26 +289,23 @@
     rhs_ref[...] = (pushed_ref[...] + incoming_flux(payload_ref, halo_refs, spread_ref, incoming_ref)).astype(BF16)
     low.wait()
     high.wait()
-
-    def bounds(t, carry):
+    expanded.wait()
+
+    def prepare(t, slot):
         for m, part in enumerate(turned(low_ref[tile(t), :])):
-            lower_ref[8 * m : 8 * m + 8, tile(t)] = part
+            lower_refs[slot][8 * m : 8 * m + 8, :] = part
         for m, part in enumerate(turned(high_ref[tile(t), :])):
-            upper_ref[8 * m : 8 * m + 8, tile(t)] = part
-        return carry
-
-    lax.fori_loop(0, TILES, bounds, 0)
-    expanded.wait()
-
-    def emit(t, m, part):
+            upper_refs[slot][8 * m : 8 * m + 8, :] = part
+
+    def emit(t, slot, m, part):
         rows = slice(8 * m, 8 * m + 8)
         moved = u_ref[rows, tile(t)] + part
-        next_ref[rows, tile(t)] = jnp.minimum(jnp.maximum(moved, lower_ref[rows, tile(t)]), upper_ref[rows, tile(t)])
+        next_ref[rows, tile(t)] = jnp.minimum(jnp.maximum(moved, lower_refs[slot][rows, :]), upper_refs[slot][rows, :])
 
     def wait(t):
         fetch_tile(sources[0], matrix_ref, sems, t).wait()
 
-    apply_matrices(wait, matrix_ref, rhs_ref, expand_ref, left_ref, product_ref, emit)
+    apply_matrices(wait, prepare, matrix_ref, rhs_ref, expand_ref, left_refs, product_refs, emit)
     table.wait()
     return table_ref[...]
 
@@ -311,7 +323,7 @@
     sources, fields, halo_refs, slot_ref, refs = refs[:5], refs[5:9], refs[9:15], refs[15], refs[16:]
     outgoing_ref, next_ref, scratch = refs[0], refs[1], refs[2:]
     order = update(sources, fields, halo_refs, next_ref, scratch)
-    chunk = 256
+    chunk = 512
     slot = slot_ref[...]
     work = dot(order, next_ref[...].astype(BF16)).astype(BF16)
 
@@ -332,14 +344,14 @@
 WORK = pltpu.VMEM((WIDTH, ZONES), BF16)
 PAYLOAD = pltpu.VMEM((6 * FACE, ZONES), BF16)
 APPLY_SCRATCH = [
-    pltpu.VMEM((8 * ZONES, TILE), F32),
-    pltpu.VMEM((TILE // GROUP * 8, DOFS // 2 * GROUP), F32),
+    *[pltpu.VMEM((8 * TILE, TILE), F32)] * 2,
+    *[pltpu.VMEM((TILE // GROUP * 8, DOFS // 2 * GROUP), F32)] * 2,
     pltpu.VMEM((ZONES, DOFS * DOFS), BF16),
     pltpu.VMEM((WIDTH, 2 * WIDTH), BF16),
     pltpu.SemaphoreType.DMA((TILES + 4,)),
 ]
 ROWMAJOR = pltpu.VMEM((ZONES, WIDTH), F32)
-UPDATE_SCRATCH = [PAYLOAD, WORK, *APPLY_SCRATCH, STATE, STATE, ROWMAJOR, ROWMAJOR]
+UPDATE_SCRATCH = [PAYLOAD, WORK, *APPLY_SCRATCH, *[pltpu.VMEM((WIDTH, TILE), F32)] * 4, ROWMAJOR, ROWMAJOR]
 
 
 def call(kernel, name, sources, args, out_shape, scratch_shapes, limit):

time: 86.9 us -> 77.2 us (0.89)
  Pallas kernels: 41.7 us -> 32 us
    pallas_call x5, Pallas kernels: 41.7 us -> 32 us  [call(): pl.pallas_call(kernel, in_specs=[pl.BlockSpec(memory_space=pltpu.HBM)] *...]
  transfers between devices with their start and end apart: 12 -> 12, of which waited for: 0 -> 0; matrix products, arithmetic and copies ran while one was open for 0% -> 0% of each run, Pallas kernels for 18% -> 15%
where the time goes in v3:
time: 77.2 us; the launch traced here: 77 us
  Pallas kernels  32 us (41%)
  blocking collectives  24.9 us (32%)
  starting transfers between devices  18.4 us (24%)
  other arithmetic  1.55 us (2%)
    pallas_call x5, Pallas kernels, call(): pl.pallas_call(kernel, in_specs=[pl.BlockSpec(memory_space=pltpu.HBM)] *...  32 us
    all_to_all x1, blocking collectives, shards(): lax.all_to_all(outgoing.reshape(devices, CAP, WIDTH), AXES, split_axis=0,...  24.9 us
    ppermute x12, starting transfers between devices, exchange(): lax.ppermute(send, axis, [(i, (i + move) % count) for i in range(count)])  18.4 us
    convert_element_type x1, other arithmetic, shards(): return arrived.reshape(devices * CAP, WIDTH).astype(F32)  1.55 us
  transfers between devices with their start and end apart: 12, of which 0 were waited for; matrix products, arithmetic and copies ran while one was open for 0% of the time, Pallas kernels for 15%

profile of v3, /device:TPU:1, one launch (start us, length us, event | category | flops | bytes accessed | tf_op | source)
XLA Modules:
  0.0 77.0 jit_solution(18098968359896525360)
XLA Ops:
  0.0 2.7 %begin.1 = (f32[256,1024]{1,0:T(8,128)S(1)}, bf16[256,1024]{1,0:T(8,128)(2,1)S(1)}, bf16[384,1024]{1,0:T(8,128)(2,1)S(1)}, s32[1,1024]{1,0:T(1,128)S(1)}, bf16[2...) custom-call(f32[1024,256]{1,0:T(8,128)} %bitcast.20, ...), custom_call_target="tpu_custom_call" | custom-call | tf_op jit(solution)/shard_map/begin/pallas_call | solution.py:360
  2.7 2.5 %collective-permute-start.2 = (bf16[64,128]{1,0:T(8,128)(2,1)S(1)}, bf16[64,128]{1,0:T(8,128)(2,1)S(1)}, u32[]{:S(2)}, u32[]{:S(2)}) collective-permute-start(bf16[64,128]{1,0:T(8,128)(2,1)S(1)} %get-tuple-element.31), channel_id=1, source_target_pairs={{0,8},{8,16},{16,24},{24,0},{1,9},{9,17},{17,25},{25,1},{2,10},{10... | collective-permute-start | bytes 49160 | tf_op jit(solution)/shard_map/ppermute | solution.py:376
  5.3 1.2 %collective-permute-start = (bf16[64,256]{1,0:T(8,128)(2,1)S(1)}, bf16[64,256]{1,0:T(8,128)(2,1)S(1)}, u32[]{:S(2)}, u32[]{:S(2)}) collective-permute-start(bf16[64,256]{1,0:T(8,128)(2,1)S(1)} %get-tuple-element.29), channel_id=1, source_target_pairs={{0,32},{32,64},{64,96},{96,0},{1,33},{33,65},{65,97},{97,1},{2,34}... | collective-permute-start | bytes 98312 | tf_op jit(solution)/shard_map/ppermute | solution.py:376
  6.5 1.5 %collective-permute-start.1 = (bf16[64,256]{1,0:T(8,128)(2,1)S(1)}, bf16[64,256]{1,0:T(8,128)(2,1)S(1)}, u32[]{:S(2)}, u32[]{:S(2)}) collective-permute-start(bf16[64,256]{1,0:T(8,128)(2,1)S(1)} %get-tuple-element.30), channel_id=1, source_target_pairs={{0,96},{32,0},{64,32},{96,64},{1,97},{33,1},{65,33},{97,65},{2,98}... | collective-permute-start | bytes 98312 | tf_op jit(solution)/shard_map/ppermute | solution.py:376
  7.9 2.2 %collective-permute-start.3 = (bf16[64,128]{1,0:T(8,128)(2,1)S(1)}, bf16[64,128]{1,0:T(8,128)(2,1)S(1)}, u32[]{:S(2)}, u32[]{:S(2)}) collective-permute-start(bf16[64,128]{1,0:T(8,128)(2,1)S(1)} %get-tuple-element.32), channel_id=1, source_target_pairs={{0,24},{8,0},{16,8},{24,16},{1,25},{9,1},{17,9},{25,17},{2,26},{10... | collective-permute-start | bytes 49160 | tf_op jit(solution)/shard_map/ppermute | solution.py:376
  10.1 2.7 %collective-permute-start.4 = (bf16[64,128]{1,0:T(8,128)(2,1)S(1)}, bf16[64,128]{1,0:T(8,128)(2,1)S(1)}, u32[]{:S(2)}, u32[]{:S(2)}) collective-permute-start(bf16[64,128]{1,0:T(8,128)(2,1)S(1)} %get-tuple-element.33), channel_id=1, source_target_pairs={{0,1},{1,2},{2,3},{3,4},{4,5},{5,6},{6,7},{7,0},{8,9},{9,10},{10,1... | collective-permute-start | bytes 49160 | tf_op jit(solution)/shard_map/ppermute | solution.py:376
  12.8 0.0 collective-permute-done.2.refs_11_
  12.8 0.0 collective-permute-start.5
  12.8 5.7 %push.2.refs_6_ = f32[256,1024]{1,0:T(8,128)S(1)} custom-call(bf16[1024,4096]{1,0:T(8,128)(2,1)} %bitcast.12, bf16[256,512]{1,0:T(8,128)(2,1)} %constant.11.clone.expand_source.refs_3_, bf16[256,1024]{1,0:T(8,128)(2,1)S(1)} %get-tuple-element.26.work_ref), custom_call_target="tpu_custom_call" | custom-call | tf_op jit(solution)/shard_map/push/pallas_call | solution.py:360
  18.5 0.0 collective-permute-done.3.refs_12_
  18.5 0.0 collective-permute-done.4.refs_13_
  18.6 0.0 collective-permute-done.5.refs_14_
  18.6 0.0 collective-permute-done.refs_9_
  18.6 0.0 collective-permute-done.1.refs_10_
  18.6 8.1 %step_on.1 = (f32[256,1024]{1,0:T(8,128)S(1)}, bf16[256,1024]{1,0:T(8,128)(2,1)S(1)}, bf16[384,1024]{1,0:T(8,128)(2,1)S(1)}, bf16[64,256]{1,0:T(8,128)(2,1)S(1)}...) custom-call(bf16[1024,4096]{1,0:T(8,128)(2,1)} %bitcast.14, ...), custom_call_target="tpu_custom_call" | custom-call | tf_op jit(solution)/shard_map/step_on/pallas_call | solution.py:360
  26.7 0.1 collective-permute-start.8
  26.7 0.1 collective-permute-start.6
  26.8 2.7 %collective-permute-start.7 = (bf16[64,256]{1,0:T(8,128)(2,1)S(1)}, bf16[64,256]{1,0:T(8,128)(2,1)S(1)}, u32[]{:S(2)}, u32[]{:S(2)}) collective-permute-start(bf16[64,256]{1,0:T(8,128)(2,1)S(1)} %get-tuple-element.39), channel_id=1, source_target_pairs={{0,96},{32,0},{64,32},{96,64},{1,97},{33,1},{65,33},{97,65},{2,98}... | collective-permute-start | bytes 98312 | tf_op jit(solution)/shard_map/ppermute | solution.py:376
  29.5 2.6 %collective-permute-start.9 = (bf16[64,128]{1,0:T(8,128)(2,1)S(1)}, bf16[64,128]{1,0:T(8,128)(2,1)S(1)}, u32[]{:S(2)}, u32[]{:S(2)}) collective-permute-start(bf16[64,128]{1,0:T(8,128)(2,1)S(1)} %get-tuple-element.41), channel_id=1, source_target_pairs={{0,24},{8,0},{16,8},{24,16},{1,25},{9,1},{17,9},{25,17},{2,26},{10... | collective-permute-start | bytes 49160 | tf_op jit(solution)/shard_map/ppermute | solution.py:376
  32.1 2.9 %collective-permute-start.10 = (bf16[64,128]{1,0:T(8,128)(2,1)S(1)}, bf16[64,128]{1,0:T(8,128)(2,1)S(1)}, u32[]{:S(2)}, u32[]{:S(2)}) collective-permute-start(bf16[64,128]{1,0:T(8,128)(2,1)S(1)} %get-tuple-element.42), channel_id=1, source_target_pairs={{0,1},{1,2},{2,3},{3,4},{4,5},{5,6},{6,7},{7,0},{8,9},{9,10},{10,1... | collective-permute-start | bytes 49160 | tf_op jit(solution)/shard_map/ppermute | solution.py:376
  35.0 0.0 collective-permute-done.8.refs_11_
  35.0 0.0 collective-permute-start.11
  35.0 5.7 %push.3.refs_6_ = f32[256,1024]{1,0:T(8,128)S(1)} custom-call(bf16[1024,4096]{1,0:T(8,128)(2,1)} %bitcast.13, bf16[256,512]{1,0:T(8,128)(2,1)} %constant.11.clone.expand_source.refs_3_, bf16[256,1024]{1,0:T(8,128)(2,1)S(1)} %get-tuple-element.36.work_ref), custom_call_target="tpu_custom_call" | custom-call | tf_op jit(solution)/shard_map/push/pallas_call | solution.py:360
  40.7 0.0 collective-permute-done.9.refs_12_
  40.7 0.0 collective-permute-done.10.refs_13_
  40.7 0.0 collective-permute-done.11.refs_14_
  40.7 0.0 collective-permute-done.6.refs_9_
  40.7 0.0 collective-permute-done.7.refs_10_
  40.8 9.8 %finish.1 = bf16[2048,256]{1,0:T(8,128)(2,1)S(1)} custom-call(bf16[1024,4096]{1,0:T(8,128)(2,1)} %bitcast.15, f32[1024,256]{1,0:T(8,128)} %bitcast.17, f32[1024,256]{1,0:T(8,128)} %bitcast.19, bf16[256,512]{1,0:T(8,128)(2,1)} %constant.11.clone.expand_source.refs_3_, bf16[256,256]{1,0:T(8,128)(2,1)} %constant.12.clone.refs_4_, ...), custom_call_target="tpu_custom_call" | custom-call | tf_op jit(solution)/shard_map/finish/pallas_call | solution.py:360
  50.6 24.9 %all_to_all.5 = bf16[128,16,256]{2,1,0:T(8,128)(2,1)S(1)} all-to-all(bf16[128,16,256]{2,1,0:T(8,128)(2,1)S(1)} %bitcast.11), channel_id=1, replica_groups=mesh['gx'=4,'gy'=4,'gz'=8] {'gx','gy','gz'}, dimensions={0} | all-to-all | bytes 2097152 | tf_op jit(solution)/shard_map/all_to_all | solution.py:427
  75.5 1.5 %bitcast_convert_fusion = f32[2048,256]{1,0:T(8,128)} fusion(bf16[128,16,256]{2,1,0:T(8,128)(2,1)S(1)} %all_to_all.5), kind=kLoop, calls=%fused_computation | loop fusion | flops 524288 | bytes 3145728 | tf_op jit(solution)/shard_map/convert_element_type | solution.py:428
Async XLA Ops:
  2.7 10.1 %collective-permute-start.2 = (bf16[64,128]{1,0:T(8,128)(2,1)S(1)}, bf16[64,128]{1,0:T(8,128)(2,1)S(1)}, u32[]{:S(2)}, u32[]{:S(2)}) collective-permute-start(bf16[64,128]{1,0:T(8,128)(2,1)S(1)} %get-tuple-element.31), channel_id=1, source_target_pairs={{0,8},{8,16},{16,24},{24,0},{1,9},{9,17},{17,25},{25,1},{2,10},{10... | collective-permute-start | bytes 49160 | tf_op jit(solution)/shard_map/ppermute | solution.py:376
  5.3 13.3 %collective-permute-start = (bf16[64,256]{1,0:T(8,128)(2,1)S(1)}, bf16[64,256]{1,0:T(8,128)(2,1)S(1)}, u32[]{:S(2)}, u32[]{:S(2)}) collective-permute-start(bf16[64,256]{1,0:T(8,128)(2,1)S(1)} %get-tuple-element.29), channel_id=1, source_target_pairs={{0,32},{32,64},{64,96},{96,0},{1,33},{33,65},{65,97},{97,1},{2,34}... | collective-permute-start | bytes 98312 | tf_op jit(solution)/shard_map/ppermute | solution.py:376
  6.5 12.1 %collective-permute-start.1 = (bf16[64,256]{1,0:T(8,128)(2,1)S(1)}, bf16[64,256]{1,0:T(8,128)(2,1)S(1)}, u32[]{:S(2)}, u32[]{:S(2)}) collective-permute-start(bf16[64,256]{1,0:T(8,128)(2,1)S(1)} %get-tuple-element.30), channel_id=1, source_target_pairs={{0,96},{32,0},{64,32},{96,64},{1,97},{33,1},{65,33},{97,65},{2,98}... | collective-permute-start | bytes 98312 | tf_op jit(solution)/shard_map/ppermute | solution.py:376
  7.9 10.6 %collective-permute-start.3 = (bf16[64,128]{1,0:T(8,128)(2,1)S(1)}, bf16[64,128]{1,0:T(8,128)(2,1)S(1)}, u32[]{:S(2)}, u32[]{:S(2)}) collective-permute-start(bf16[64,128]{1,0:T(8,128)(2,1)S(1)} %get-tuple-element.32), channel_id=1, source_target_pairs={{0,24},{8,0},{16,8},{24,16},{1,25},{9,1},{17,9},{25,17},{2,26},{10... | collective-permute-start | bytes 49160 | tf_op jit(solution)/shard_map/ppermute | solution.py:376
  10.1 8.4 %collective-permute-start.4 = (bf16[64,128]{1,0:T(8,128)(2,1)S(1)}, bf16[64,128]{1,0:T(8,128)(2,1)S(1)}, u32[]{:S(2)}, u32[]{:S(2)}) collective-permute-start(bf16[64,128]{1,0:T(8,128)(2,1)S(1)} %get-tuple-element.33), channel_id=1, source_target_pairs={{0,1},{1,2},{2,3},{3,4},{4,5},{5,6},{6,7},{7,0},{8,9},{9,10},{10,1... | collective-permute-start | bytes 49160 | tf_op jit(solution)/shard_map/ppermute | solution.py:376
  12.8 5.7 %collective-permute-start.5 = (bf16[64,128]{1,0:T(8,128)(2,1)S(1)}, bf16[64,128]{1,0:T(8,128)(2,1)S(1)}, u32[]{:S(2)}, u32[]{:S(2)}) collective-permute-start(bf16[64,128]{1,0:T(8,128)(2,1)S(1)} %get-tuple-element.34), channel_id=1, source_target_pairs={{0,7},{1,0},{2,1},{3,2},{4,3},{5,4},{6,5},{7,6},{8,15},{9,8},{10,9... | collective-permute-start | bytes 49160 | tf_op jit(solution)/shard_map/ppermute | solution.py:376
  26.7 8.3 %collective-permute-start.8 = (bf16[64,128]{1,0:T(8,128)(2,1)S(1)}, bf16[64,128]{1,0:T(8,128)(2,1)S(1)}, u32[]{:S(2)}, u32[]{:S(2)}) collective-permute-start(bf16[64,128]{1,0:T(8,128)(2,1)S(1)} %get-tuple-element.40), channel_id=1, source_target_pairs={{0,8},{8,16},{16,24},{24,0},{1,9},{9,17},{17,25},{25,1},{2,10},{10... | collective-permute-start | bytes 49160 | tf_op jit(solution)/shard_map/ppermute | solution.py:376
  26.7 14.0 %collective-permute-start.6 = (bf16[64,256]{1,0:T(8,128)(2,1)S(1)}, bf16[64,256]{1,0:T(8,128)(2,1)S(1)}, u32[]{:S(2)}, u32[]{:S(2)}) collective-permute-start(bf16[64,256]{1,0:T(8,128)(2,1)S(1)} %get-tuple-element.38), channel_id=1, source_target_pairs={{0,32},{32,64},{64,96},{96,0},{1,33},{33,65},{65,97},{97,1},{2,34}... | collective-permute-start | bytes 98312 | tf_op jit(solution)/shard_map/ppermute | solution.py:376
  26.8 13.9 %collective-permute-start.7 = (bf16[64,256]{1,0:T(8,128)(2,1)S(1)}, bf16[64,256]{1,0:T(8,128)(2,1)S(1)}, u32[]{:S(2)}, u32[]{:S(2)}) collective-permute-start(bf16[64,256]{1,0:T(8,128)(2,1)S(1)} %get-tuple-element.39), channel_id=1, source_target_pairs={{0,96},{32,0},{64,32},{96,64},{1,97},{33,1},{65,33},{97,65},{2,98}... | collective-permute-start | bytes 98312 | tf_op jit(solution)/shard_map/ppermute | solution.py:376
  29.5 11.2 %collective-permute-start.9 = (bf16[64,128]{1,0:T(8,128)(2,1)S(1)}, bf16[64,128]{1,0:T(8,128)(2,1)S(1)}, u32[]{:S(2)}, u32[]{:S(2)}) collective-permute-start(bf16[64,128]{1,0:T(8,128)(2,1)S(1)} %get-tuple-element.41), channel_id=1, source_target_pairs={{0,24},{8,0},{16,8},{24,16},{1,25},{9,1},{17,9},{25,17},{2,26},{10... | collective-permute-start | bytes 49160 | tf_op jit(solution)/shard_map/ppermute | solution.py:376
  32.1 8.6 %collective-permute-start.10 = (bf16[64,128]{1,0:T(8,128)(2,1)S(1)}, bf16[64,128]{1,0:T(8,128)(2,1)S(1)}, u32[]{:S(2)}, u32[]{:S(2)}) collective-permute-start(bf16[64,128]{1,0:T(8,128)(2,1)S(1)} %get-tuple-element.42), channel_id=1, source_target_pairs={{0,1},{1,2},{2,3},{3,4},{4,5},{5,6},{6,7},{7,0},{8,9},{9,10},{10,1... | collective-permute-start | bytes 49160 | tf_op jit(solution)/shard_map/ppermute | solution.py:376
  35.0 5.8 %collective-permute-start.11 = (bf16[64,128]{1,0:T(8,128)(2,1)S(1)}, bf16[64,128]{1,0:T(8,128)(2,1)S(1)}, u32[]{:S(2)}, u32[]{:S(2)}) collective-permute-start(bf16[64,128]{1,0:T(8,128)(2,1)S(1)} %get-tuple-element.43), channel_id=1, source_target_pairs={{0,7},{1,0},{2,1},{3,2},{4,3},{5,4},{6,5},{7,6},{8,15},{9,8},{10,9... | collective-permute-start | bytes 49160 | tf_op jit(solution)/shard_map/ppermute | solution.py:376

commit v4 on v3

--- a/solution.py
+++ b/solution.py
@@ -167,7 +167,8 @@
 
 
 def apply_matrices(wait, prepare, matrix_ref, values_ref, expand_ref, left_refs, product_refs, emit):
-    zone = lax.broadcasted_iota(jnp.int32, (8, DOFS // 2 * GROUP), 1) % GROUP
+    zone = lax.broadcasted_iota(jnp.int32, (8, TILE), 1) % GROUP
+    odds = [zone & bit != 0 for bit in (1, 2, 4, 8)]
     shape = (8 * GROUP, TILE)
     half = lax.broadcasted_iota(jnp.int32, shape, 0) % 2 == lax.broadcasted_iota(jnp.int32, shape, 1) // DOFS
 
@@ -186,10 +187,12 @@
             matrix = matrix_ref[pl.ds(pl.multiple_of(t * TILE + GROUP * g, GROUP), GROUP), :]
             right = jnp.concatenate([matrix[:, TILE * m : TILE * (m + 1)] for m in range(DOFS // 2)], axis=0)
             product = lax.dot_general(left, right, (((1,), (1,)), ((), ())), preferred_element_type=F32)
-            kept = product[0:8]
-            for z in range(1, GROUP):
-                kept = jnp.where(zone == z, product[8 * z : 8 * z + 8], kept)
-            product_ref[8 * g : 8 * g + 8, :] = kept
+            for q in range(4):
+                lanes = slice(TILE * q, TILE * (q + 1))
+                kept = [product[8 * z : 8 * z + 8, lanes] for z in range(GROUP)]
+                for odd in odds:
+                    kept = [jnp.where(odd, b, a) for a, b in zip(kept[0::2], kept[1::2])]
+                product_ref[8 * g : 8 * g + 8, lanes] = kept[0]
 
     def settle(t, slot):
         product_ref = product_refs[slot]
@@ -225,17 +228,8 @@
     targets, sems = refs[17:23], refs[23]
     state_ref, pick_ref, owner_ref, coupling_ref, rows_ref, columns_ref = targets
     copies = fetches(list(zip(sources, targets)), sems)
-    for copy in copies:
+    for copy in copies[::-1]:
         copy.start()
-    copies[0].wait()
-    for t in range(TILES):
-        lanes = slice(TILE * t, TILE * (t + 1))
-        for m, part in enumerate(turned(state_ref[lanes, :])):
-            u_ref[8 * m : 8 * m + 8, lanes] = part
-    work = u_ref[...].astype(BF16)
-    work_ref[...] = work
-    copies[1].wait()
-    write_faces(work, pick_ref[...], payload_ref, send_refs)
     for copy in copies[2:]:
         copy.wait()
     before = lax.broadcasted_iota(jnp.int32, (TILE, TILE), 0) < lax.broadcasted_iota(jnp.int32, (TILE, TILE), 1)
@@ -254,6 +248,15 @@
     own = lax.broadcasted_iota(jnp.int32, entries.shape, 0) // 2 % COMP
     theirs = lax.broadcasted_iota(jnp.int32, entries.shape, 1) // 16 % COMP
     spread_ref[...] = jnp.where(own == theirs, entries, 0.0).astype(BF16)
+    copies[0].wait()
+    for t in range(TILES):
+        lanes = slice(TILE * t, TILE * (t + 1))
+        for m, part in enumerate(turned(state_ref[lanes, :])):
+            u_ref[8 * m : 8 * m + 8, lanes] = part
+    work = u_ref[...].astype(BF16)
+    work_ref[...] = work
+    copies[1].wait()
+    write_faces(work, pick_ref[...], payload_ref, send_refs)
 
 
 def push_kernel(matrix_source, expand_source, work_ref, pushed_ref, *scratch):
@@ -339,7 +342,7 @@
 
 
 INNER = pl.BlockSpec(memory_space=pltpu.VMEM)
-SEND_SHAPES = [jax.ShapeDtypeStruct(s, BF16) for s in SENDS]
+SEND_SHAPES = [pltpu.VMEM(s, BF16) for s in SENDS]
 STATE = pltpu.VMEM((WIDTH, ZONES), F32)
 WORK = pltpu.VMEM((WIDTH, ZONES), BF16)
 PAYLOAD = pltpu.VMEM((6 * FACE, ZONES), BF16)

time: 77.2 us -> 76.9 us (level)
  no operation moved by 1% of the time
where the time goes in v4:
time: 76.9 us; the launch traced here: 76.7 us
  Pallas kernels  31.7 us (41%)
  blocking collectives  24.9 us (32%)
  starting transfers between devices  18.4 us (24%)
  other arithmetic  1.55 us (2%)
    pallas_call x5, Pallas kernels, call(): pl.pallas_call(kernel, in_specs=[pl.BlockSpec(memory_space=pltpu.HBM)] *...  31.7 us
    all_to_all x1, blocking collectives, shards(): lax.all_to_all(outgoing.reshape(devices, CAP, WIDTH), AXES, split_axis=0,...  24.9 us
    ppermute x12, starting transfers between devices, exchange(): lax.ppermute(send, axis, [(i, (i + move) % count) for i in range(count)])  18.4 us
    convert_element_type x1, other arithmetic, shards(): return arrived.reshape(devices * CAP, WIDTH).astype(F32)  1.55 us
  transfers between devices with their start and end apart: 12, of which 0 were waited for; matrix products, arithmetic and copies ran while one was open for 0% of the time, Pallas kernels for 15%

profile of v4, /device:TPU:1, one launch (start us, length us, event | category | flops | bytes accessed | tf_op | source)
XLA Modules:
  0.0 76.7 jit_solution(18421490169827186132)
XLA Ops:
  0.0 2.5 %begin.1 = (f32[256,1024]{1,0:T(8,128)S(1)}, bf16[256,1024]{1,0:T(8,128)(2,1)S(1)}, bf16[384,1024]{1,0:T(8,128)(2,1)S(1)}, s32[1,1024]{1,0:T(1,128)S(1)}, bf16[2...) custom-call(f32[1024,256]{1,0:T(8,128)} %bitcast.20, ...), custom_call_target="tpu_custom_call" | custom-call | tf_op jit(solution)/shard_map/begin/pallas_call | solution.py:363
  2.5 2.5 %collective-permute-start.2 = (bf16[64,128]{1,0:T(8,128)(2,1)S(1)}, bf16[64,128]{1,0:T(8,128)(2,1)S(1)}, u32[]{:S(2)}, u32[]{:S(2)}) collective-permute-start(bf16[64,128]{1,0:T(8,128)(2,1)S(1)} %get-tuple-element.31), channel_id=1, source_target_pairs={{0,8},{8,16},{16,24},{24,0},{1,9},{9,17},{17,25},{25,1},{2,10},{10... | collective-permute-start | bytes 49160 | tf_op jit(solution)/shard_map/ppermute | solution.py:379
  5.0 1.2 %collective-permute-start = (bf16[64,256]{1,0:T(8,128)(2,1)S(1)}, bf16[64,256]{1,0:T(8,128)(2,1)S(1)}, u32[]{:S(2)}, u32[]{:S(2)}) collective-permute-start(bf16[64,256]{1,0:T(8,128)(2,1)S(1)} %get-tuple-element.29), channel_id=1, source_target_pairs={{0,32},{32,64},{64,96},{96,0},{1,33},{33,65},{65,97},{97,1},{2,34}... | collective-permute-start | bytes 98312 | tf_op jit(solution)/shard_map/ppermute | solution.py:379
  6.2 1.5 %collective-permute-start.1 = (bf16[64,256]{1,0:T(8,128)(2,1)S(1)}, bf16[64,256]{1,0:T(8,128)(2,1)S(1)}, u32[]{:S(2)}, u32[]{:S(2)}) collective-permute-start(bf16[64,256]{1,0:T(8,128)(2,1)S(1)} %get-tuple-element.30), channel_id=1, source_target_pairs={{0,96},{32,0},{64,32},{96,64},{1,97},{33,1},{65,33},{97,65},{2,98}... | collective-permute-start | bytes 98312 | tf_op jit(solution)/shard_map/ppermute | solution.py:379
  7.7 2.2 %collective-permute-start.3 = (bf16[64,128]{1,0:T(8,128)(2,1)S(1)}, bf16[64,128]{1,0:T(8,128)(2,1)S(1)}, u32[]{:S(2)}, u32[]{:S(2)}) collective-permute-start(bf16[64,128]{1,0:T(8,128)(2,1)S(1)} %get-tuple-element.32), channel_id=1, source_target_pairs={{0,24},{8,0},{16,8},{24,16},{1,25},{9,1},{17,9},{25,17},{2,26},{10... | collective-permute-start | bytes 49160 | tf_op jit(solution)/shard_map/ppermute | solution.py:379
  9.9 2.7 %collective-permute-start.4 = (bf16[64,128]{1,0:T(8,128)(2,1)S(1)}, bf16[64,128]{1,0:T(8,128)(2,1)S(1)}, u32[]{:S(2)}, u32[]{:S(2)}) collective-permute-start(bf16[64,128]{1,0:T(8,128)(2,1)S(1)} %get-tuple-element.33), channel_id=1, source_target_pairs={{0,1},{1,2},{2,3},{3,4},{4,5},{5,6},{6,7},{7,0},{8,9},{9,10},{10,1... | collective-permute-start | bytes 49160 | tf_op jit(solution)/shard_map/ppermute | solution.py:379
  12.6 0.0 collective-permute-done.2.refs_11_
  12.6 0.0 collective-permute-start.5
  12.6 5.7 %push.2.refs_6_ = f32[256,1024]{1,0:T(8,128)S(1)} custom-call(bf16[1024,4096]{1,0:T(8,128)(2,1)} %bitcast.12, bf16[256,512]{1,0:T(8,128)(2,1)} %constant.11.clone.expand_source.refs_3_, bf16[256,1024]{1,0:T(8,128)(2,1)S(1)} %get-tuple-element.26.work_ref), custom_call_target="tpu_custom_call" | custom-call | tf_op jit(solution)/shard_map/push/pallas_call | solution.py:363
  18.3 0.0 collective-permute-done.3.refs_12_
  18.4 0.0 collective-permute-done.4.refs_13_
  18.4 0.0 collective-permute-done.5.refs_14_
  18.4 0.0 collective-permute-done.refs_9_
  18.4 0.0 collective-permute-done.1.refs_10_
  18.4 8.0 %step_on.1 = (f32[256,1024]{1,0:T(8,128)S(1)}, bf16[256,1024]{1,0:T(8,128)(2,1)S(1)}, bf16[384,1024]{1,0:T(8,128)(2,1)S(1)}, bf16[64,256]{1,0:T(8,128)(2,1)S(1)}...) custom-call(bf16[1024,4096]{1,0:T(8,128)(2,1)} %bitcast.14, ...), custom_call_target="tpu_custom_call" | custom-call | tf_op jit(solution)/shard_map/step_on/pallas_call | solution.py:363
  26.4 0.1 collective-permute-start.8
  26.5 0.1 collective-permute-start.6
  26.6 2.7 %collective-permute-start.7 = (bf16[64,256]{1,0:T(8,128)(2,1)S(1)}, bf16[64,256]{1,0:T(8,128)(2,1)S(1)}, u32[]{:S(2)}, u32[]{:S(2)}) collective-permute-start(bf16[64,256]{1,0:T(8,128)(2,1)S(1)} %get-tuple-element.39), channel_id=1, source_target_pairs={{0,96},{32,0},{64,32},{96,64},{1,97},{33,1},{65,33},{97,65},{2,98}... | collective-permute-start | bytes 98312 | tf_op jit(solution)/shard_map/ppermute | solution.py:379
  29.3 2.6 %collective-permute-start.9 = (bf16[64,128]{1,0:T(8,128)(2,1)S(1)}, bf16[64,128]{1,0:T(8,128)(2,1)S(1)}, u32[]{:S(2)}, u32[]{:S(2)}) collective-permute-start(bf16[64,128]{1,0:T(8,128)(2,1)S(1)} %get-tuple-element.41), channel_id=1, source_target_pairs={{0,24},{8,0},{16,8},{24,16},{1,25},{9,1},{17,9},{25,17},{2,26},{10... | collective-permute-start | bytes 49160 | tf_op jit(solution)/shard_map/ppermute | solution.py:379
  31.9 2.8 %collective-permute-start.10 = (bf16[64,128]{1,0:T(8,128)(2,1)S(1)}, bf16[64,128]{1,0:T(8,128)(2,1)S(1)}, u32[]{:S(2)}, u32[]{:S(2)}) collective-permute-start(bf16[64,128]{1,0:T(8,128)(2,1)S(1)} %get-tuple-element.42), channel_id=1, source_target_pairs={{0,1},{1,2},{2,3},{3,4},{4,5},{5,6},{6,7},{7,0},{8,9},{9,10},{10,1... | collective-permute-start | bytes 49160 | tf_op jit(solution)/shard_map/ppermute | solution.py:379
  34.7 0.0 collective-permute-done.8.refs_11_
  34.7 0.1 collective-permute-start.11
  34.8 5.7 %push.3.refs_6_ = f32[256,1024]{1,0:T(8,128)S(1)} custom-call(bf16[1024,4096]{1,0:T(8,128)(2,1)} %bitcast.13, bf16[256,512]{1,0:T(8,128)(2,1)} %constant.11.clone.expand_source.refs_3_, bf16[256,1024]{1,0:T(8,128)(2,1)S(1)} %get-tuple-element.36.work_ref), custom_call_target="tpu_custom_call" | custom-call | tf_op jit(solution)/shard_map/push/pallas_call | solution.py:363
  40.5 0.0 collective-permute-done.9.refs_12_
  40.5 0.0 collective-permute-done.10.refs_13_
  40.5 0.0 collective-permute-done.11.refs_14_
  40.5 0.0 collective-permute-done.6.refs_9_
  40.5 0.0 collective-permute-done.7.refs_10_
  40.5 9.7 %finish.1 = bf16[2048,256]{1,0:T(8,128)(2,1)S(1)} custom-call(bf16[1024,4096]{1,0:T(8,128)(2,1)} %bitcast.15, f32[1024,256]{1,0:T(8,128)} %bitcast.17, f32[1024,256]{1,0:T(8,128)} %bitcast.19, bf16[256,512]{1,0:T(8,128)(2,1)} %constant.11.clone.expand_source.refs_3_, bf16[256,256]{1,0:T(8,128)(2,1)} %constant.12.clone.refs_4_, ...), custom_call_target="tpu_custom_call" | custom-call | tf_op jit(solution)/shard_map/finish/pallas_call | solution.py:363
  50.3 24.9 %all_to_all.5 = bf16[128,16,256]{2,1,0:T(8,128)(2,1)S(1)} all-to-all(bf16[128,16,256]{2,1,0:T(8,128)(2,1)S(1)} %bitcast.11), channel_id=1, replica_groups=mesh['gx'=4,'gy'=4,'gz'=8] {'gx','gy','gz'}, dimensions={0} | all-to-all | bytes 2097152 | tf_op jit(solution)/shard_map/all_to_all | solution.py:430
  75.1 1.5 %bitcast_convert_fusion = f32[2048,256]{1,0:T(8,128)} fusion(bf16[128,16,256]{2,1,0:T(8,128)(2,1)S(1)} %all_to_all.5), kind=kLoop, calls=%fused_computation | loop fusion | flops 524288 | bytes 3145728 | tf_op jit(solution)/shard_map/convert_element_type | solution.py:431
Async XLA Ops:
  2.5 10.1 %collective-permute-start.2 = (bf16[64,128]{1,0:T(8,128)(2,1)S(1)}, bf16[64,128]{1,0:T(8,128)(2,1)S(1)}, u32[]{:S(2)}, u32[]{:S(2)}) collective-permute-start(bf16[64,128]{1,0:T(8,128)(2,1)S(1)} %get-tuple-element.31), channel_id=1, source_target_pairs={{0,8},{8,16},{16,24},{24,0},{1,9},{9,17},{17,25},{25,1},{2,10},{10... | collective-permute-start | bytes 49160 | tf_op jit(solution)/shard_map/ppermute | solution.py:379
  5.0 13.3 %collective-permute-start = (bf16[64,256]{1,0:T(8,128)(2,1)S(1)}, bf16[64,256]{1,0:T(8,128)(2,1)S(1)}, u32[]{:S(2)}, u32[]{:S(2)}) collective-permute-start(bf16[64,256]{1,0:T(8,128)(2,1)S(1)} %get-tuple-element.29), channel_id=1, source_target_pairs={{0,32},{32,64},{64,96},{96,0},{1,33},{33,65},{65,97},{97,1},{2,34}... | collective-permute-start | bytes 98312 | tf_op jit(solution)/shard_map/ppermute | solution.py:379
  6.2 12.1 %collective-permute-start.1 = (bf16[64,256]{1,0:T(8,128)(2,1)S(1)}, bf16[64,256]{1,0:T(8,128)(2,1)S(1)}, u32[]{:S(2)}, u32[]{:S(2)}) collective-permute-start(bf16[64,256]{1,0:T(8,128)(2,1)S(1)} %get-tuple-element.30), channel_id=1, source_target_pairs={{0,96},{32,0},{64,32},{96,64},{1,97},{33,1},{65,33},{97,65},{2,98}... | collective-permute-start | bytes 98312 | tf_op jit(solution)/shard_map/ppermute | solution.py:379
  7.7 10.6 %collective-permute-start.3 = (bf16[64,128]{1,0:T(8,128)(2,1)S(1)}, bf16[64,128]{1,0:T(8,128)(2,1)S(1)}, u32[]{:S(2)}, u32[]{:S(2)}) collective-permute-start(bf16[64,128]{1,0:T(8,128)(2,1)S(1)} %get-tuple-element.32), channel_id=1, source_target_pairs={{0,24},{8,0},{16,8},{24,16},{1,25},{9,1},{17,9},{25,17},{2,26},{10... | collective-permute-start | bytes 49160 | tf_op jit(solution)/shard_map/ppermute | solution.py:379
  9.9 8.4 %collective-permute-start.4 = (bf16[64,128]{1,0:T(8,128)(2,1)S(1)}, bf16[64,128]{1,0:T(8,128)(2,1)S(1)}, u32[]{:S(2)}, u32[]{:S(2)}) collective-permute-start(bf16[64,128]{1,0:T(8,128)(2,1)S(1)} %get-tuple-element.33), channel_id=1, source_target_pairs={{0,1},{1,2},{2,3},{3,4},{4,5},{5,6},{6,7},{7,0},{8,9},{9,10},{10,1... | collective-permute-start | bytes 49160 | tf_op jit(solution)/shard_map/ppermute | solution.py:379
  12.6 5.7 %collective-permute-start.5 = (bf16[64,128]{1,0:T(8,128)(2,1)S(1)}, bf16[64,128]{1,0:T(8,128)(2,1)S(1)}, u32[]{:S(2)}, u32[]{:S(2)}) collective-permute-start(bf16[64,128]{1,0:T(8,128)(2,1)S(1)} %get-tuple-element.34), channel_id=1, source_target_pairs={{0,7},{1,0},{2,1},{3,2},{4,3},{5,4},{6,5},{7,6},{8,15},{9,8},{10,9... | collective-permute-start | bytes 49160 | tf_op jit(solution)/shard_map/ppermute | solution.py:379
  26.4 8.3 %collective-permute-start.8 = (bf16[64,128]{1,0:T(8,128)(2,1)S(1)}, bf16[64,128]{1,0:T(8,128)(2,1)S(1)}, u32[]{:S(2)}, u32[]{:S(2)}) collective-permute-start(bf16[64,128]{1,0:T(8,128)(2,1)S(1)} %get-tuple-element.40), channel_id=1, source_target_pairs={{0,8},{8,16},{16,24},{24,0},{1,9},{9,17},{17,25},{25,1},{2,10},{10... | collective-permute-start | bytes 49160 | tf_op jit(solution)/shard_map/ppermute | solution.py:379
  26.5 14.0 %collective-permute-start.6 = (bf16[64,256]{1,0:T(8,128)(2,1)S(1)}, bf16[64,256]{1,0:T(8,128)(2,1)S(1)}, u32[]{:S(2)}, u32[]{:S(2)}) collective-permute-start(bf16[64,256]{1,0:T(8,128)(2,1)S(1)} %get-tuple-element.38), channel_id=1, source_target_pairs={{0,32},{32,64},{64,96},{96,0},{1,33},{33,65},{65,97},{97,1},{2,34}... | collective-permute-start | bytes 98312 | tf_op jit(solution)/shard_map/ppermute | solution.py:379
  26.6 13.9 %collective-permute-start.7 = (bf16[64,256]{1,0:T(8,128)(2,1)S(1)}, bf16[64,256]{1,0:T(8,128)(2,1)S(1)}, u32[]{:S(2)}, u32[]{:S(2)}) collective-permute-start(bf16[64,256]{1,0:T(8,128)(2,1)S(1)} %get-tuple-element.39), channel_id=1, source_target_pairs={{0,96},{32,0},{64,32},{96,64},{1,97},{33,1},{65,33},{97,65},{2,98}... | collective-permute-start | bytes 98312 | tf_op jit(solution)/shard_map/ppermute | solution.py:379
  29.3 11.2 %collective-permute-start.9 = (bf16[64,128]{1,0:T(8,128)(2,1)S(1)}, bf16[64,128]{1,0:T(8,128)(2,1)S(1)}, u32[]{:S(2)}, u32[]{:S(2)}) collective-permute-start(bf16[64,128]{1,0:T(8,128)(2,1)S(1)} %get-tuple-element.41), channel_id=1, source_target_pairs={{0,24},{8,0},{16,8},{24,16},{1,25},{9,1},{17,9},{25,17},{2,26},{10... | collective-permute-start | bytes 49160 | tf_op jit(solution)/shard_map/ppermute | solution.py:379
  31.9 8.6 %collective-permute-start.10 = (bf16[64,128]{1,0:T(8,128)(2,1)S(1)}, bf16[64,128]{1,0:T(8,128)(2,1)S(1)}, u32[]{:S(2)}, u32[]{:S(2)}) collective-permute-start(bf16[64,128]{1,0:T(8,128)(2,1)S(1)} %get-tuple-element.42), channel_id=1, source_target_pairs={{0,1},{1,2},{2,3},{3,4},{4,5},{5,6},{6,7},{7,0},{8,9},{9,10},{10,1... | collective-permute-start | bytes 49160 | tf_op jit(solution)/shard_map/ppermute | solution.py:379
  34.7 5.8 %collective-permute-start.11 = (bf16[64,128]{1,0:T(8,128)(2,1)S(1)}, bf16[64,128]{1,0:T(8,128)(2,1)S(1)}, u32[]{:S(2)}, u32[]{:S(2)}) collective-permute-start(bf16[64,128]{1,0:T(8,128)(2,1)S(1)} %get-tuple-element.43), channel_id=1, source_target_pairs={{0,7},{1,0},{2,1},{3,2},{4,3},{5,4},{6,5},{7,6},{8,15},{9,8},{10,9... | collective-permute-start | bytes 49160 | tf_op jit(solution)/shard_map/ppermute | solution.py:379
